TPU v7x, 128 devices: a whole 4x4x4 slice. The times are simulated.
128 devices in a mesh: req: 64 (over z, y, x), seq: 2 (over core).
Axes of the slice: x: 4, y: 4, z: 4, core: 2. Of those that a mesh axis runs over, the one named last changes fastest.
Arguments:
- tokens: bfloat16 [16384, 1536], P(('req', 'seq')), may hold values from -6 to 6
- attn_gain: float32 [1536], replicated, may hold values from 0.5 to 1.5
- w_qkv: bfloat16 [1536, 2560], replicated, may hold values from -80 to 80
- w_out: bfloat16 [1536, 1536], replicated, may hold values from -0.15625 to 0.15625
- k_cache: bfloat16 [64, 2048, 512], P('req', 'seq'), may hold values from -6 to 6
- v_cache: bfloat16 [64, 2048, 512], P('req', 'seq'), may hold values from -7.5 to 7.5
- cache_len: int32 [64], P('req'), may hold values from 1 to 2048, as said below
- ffn_gain: float32 [1536], replicated, may hold values from 0.5 to 1.5
- routes: int32 [16384, 8], P(('req', 'seq')), may hold values from 0 to 39, as said below
- route_scores: float32 [16384, 8], P(('req', 'seq')), may hold values from 0.05 to 1
- replica_slot: int32 [16384, 40], P(('req', 'seq')), may hold values from 0 to 127, as said below
- expert_up: bfloat16 [128, 1536, 1024], P(('req', 'seq')), may hold values from -2 to 2, as said below
- expert_down: bfloat16 [128, 512, 1536], P(('req', 'seq')), may hold values from -2 to 2, as said below
Outputs:
- attended: bfloat16 [16384, 1536], P(('req', 'seq'))
- stream: bfloat16 [16384, 1536], P(('req', 'seq'))
- expert_mix: bfloat16 [16384, 1536], P(('req', 'seq'))
- appended: bfloat16 [16384, 1024], P(('req', 'seq'))
Inputs may be any that keep to these rules, and one draw needn't show every extreme that they name: `routes`: each token names 8 different experts. Each slot hosts one expert, every expert at least one slot; replica_slot[t, e] is a slot hosting expert e. The 128 rows of one device (rows d * 128 to (d + 1) * 128 - 1) send at most 16 of their routes to any one slot (slot replica_slot[t, routes[t, k]]), and each device sends exactly 16 to some slot. `expert_up`: slots hosting the same expert hold equal weights. `expert_down`: slots hosting the same expert hold equal weights. `cache_len`: at least one request has exactly 2048 cached positions.
All inputs are finite; a program needn't handle non-finite values.
Results may differ from a plain program's by a relative error of at most 0.01.
Values may be sent and summed in bfloat16 or wider, within the bound.
A program may use at most 128 MiB of HBM per device.

v0:
```python
import jax
import jax.numpy as jnp
from jax import lax
from jax.sharding import PartitionSpec as P

HEADS = 24
KV_HEADS = 8
HEAD = 64
KEY_BLOCK = 128


epsilon = 1e-06
residual_scale = 0.22
score_scale = 0.015625
rope_base = 10000.0
neg_big = -1e30


def rms_scale(row_block, gain_vector):
    widened = row_block.astype(jnp.float32)
    mean_square = jnp.mean(widened * widened, axis=-1, keepdims=True)
    return (widened * lax.rsqrt(mean_square + epsilon) * gain_vector).astype(jnp.bfloat16)


def rotate(head_values, positions):
    half_width = head_values.shape[-1] // 2
    frequency = rope_base ** (-jnp.arange(half_width, dtype=jnp.float32) / half_width)
    angles = positions.astype(jnp.float32)[:, None] * frequency[None, :]
    cosine = jnp.cos(angles)[:, None, :]
    sine_part = jnp.sin(angles)[:, None, :]
    lower_half = head_values[..., :half_width]
    upper_half = head_values[..., half_width:]
    return jnp.concatenate(
        [
            lower_half * cosine - upper_half * sine_part,
            upper_half * cosine + lower_half * sine_part,
        ],
        axis=-1,
    )


def project(row_block, gain_vector, w_qkv, positions):
    normed = rms_scale(row_block, gain_vector)
    projected = jnp.dot(normed, w_qkv, preferred_element_type=jnp.float32)
    query_width = HEADS * HEAD
    key_width = KV_HEADS * HEAD
    queries = rotate(projected[:, :query_width].reshape(-1, HEADS, HEAD), positions).astype(
        jnp.bfloat16
    )
    new_keys = rotate(
        projected[:, query_width : query_width + key_width].reshape(-1, KV_HEADS, HEAD), positions
    ).astype(jnp.bfloat16)
    new_values = projected[:, query_width + key_width :].astype(jnp.bfloat16)
    return (queries, new_keys, new_values)


def fold_blocks(carried, queries, key_part, value_part, visible):
    scores = (
        jnp.einsum("rkgh,nbkh->rkgnb", queries, key_part, preferred_element_type=jnp.float32)
        * score_scale
    )
    visible_mask = visible[:, None, None, :, :]
    block_max = jnp.max(jnp.where(visible_mask, scores, neg_big), axis=-1)
    weights = jnp.where(visible_mask, jnp.exp(scores - block_max[..., None]), 0.0).astype(
        jnp.bfloat16
    )
    totals = jnp.sum(weights, axis=-1, dtype=jnp.float32)
    block_sums = jnp.einsum(
        "rkgnb,nbkh->rkgnh", weights, value_part, preferred_element_type=jnp.float32
    )
    best_score, running_total, running_sum = carried
    new_best = jnp.maximum(best_score, jnp.max(block_max, axis=-1))
    old_scale = jnp.exp(best_score - new_best)
    block_scale = jnp.exp(block_max - new_best[..., None])
    running_total = running_total * old_scale + jnp.sum(totals * block_scale, axis=-1)
    running_sum = running_sum * old_scale[..., None] + jnp.sum(
        block_sums * block_scale[..., None], axis=-2
    )
    return (new_best, running_total, running_sum)


def attend_keys(carried, queries, key_rows, value_rows, visible_of):
    block_count = key_rows.shape[0] // KEY_BLOCK
    group_size = 1
    while group_size * 2 * queries.shape[0] <= 1024 and block_count % (group_size * 2) == 0:
        group_size = group_size * 2
    turn_count = block_count // group_size
    shaped_keys = key_rows.reshape(turn_count, group_size, KEY_BLOCK, KV_HEADS, HEAD)
    shaped_values = value_rows.reshape(turn_count, group_size, KEY_BLOCK, KV_HEADS, HEAD)

    def fold_step(running, inputs):
        turn_index, key_part, value_part = inputs
        visible = visible_of(turn_index * group_size * KEY_BLOCK, group_size * KEY_BLOCK)
        visible = visible.reshape(-1, group_size, KEY_BLOCK)
        return (fold_blocks(running, queries, key_part, value_part, visible), None)

    carried, _ = lax.scan(
        fold_step, carried, (jnp.arange(turn_count, dtype=jnp.int32), shaped_keys, shaped_values)
    )
    return carried


def empty_state(row_count):
    group_size = HEADS // KV_HEADS
    return (
        jnp.full((row_count, KV_HEADS, group_size), neg_big, jnp.float32),
        jnp.zeros((row_count, KV_HEADS, group_size), jnp.float32),
        jnp.zeros((row_count, KV_HEADS, group_size, HEAD), jnp.float32),
    )


def flatten_state(carried):
    best_score, running_total, running_sum = carried
    row_count = best_score.shape[0]
    return (
        best_score.reshape(row_count, HEADS),
        running_total.reshape(row_count, HEADS),
        running_sum.reshape(row_count, HEADS * HEAD),
    )


def finish_state(flat_state):
    best_score, running_total, running_sum = flat_state
    row_count = best_score.shape[0]
    shaped = running_sum.reshape(row_count, HEADS, HEAD) / running_total[..., None]
    return shaped.astype(jnp.bfloat16).reshape(row_count, HEADS * HEAD)


def run_experts(buffer, expert_up, expert_down):
    gate_up = jnp.einsum("sjcd,jdf->sjcf", buffer, expert_up, preferred_element_type=jnp.float32)
    hidden_width = expert_down.shape[1]
    active = (jax.nn.silu(gate_up[..., :hidden_width]) * gate_up[..., hidden_width:]).astype(
        jnp.bfloat16
    )
    return jnp.einsum(
        "sjcf,jfd->sjcd", active, expert_down, preferred_element_type=jnp.float32
    ).astype(jnp.bfloat16)


def shards(
    tokens,
    attn_gain,
    w_qkv,
    w_out,
    k_cache,
    v_cache,
    cache_len,
    ffn_gain,
    routes,
    route_scores,
    replica_slot,
    expert_up,
    expert_down,
):
    row_count = tokens.shape[0]
    seq_count = lax.axis_size("seq")
    seq_index = lax.axis_index("seq")
    length = cache_len[0]
    group_size = HEADS // KV_HEADS
    key_width = KV_HEADS * HEAD
    query_index = seq_index * row_count + jnp.arange(row_count, dtype=jnp.int32)
    positions = length + query_index
    queries, new_keys, new_values = project(tokens, attn_gain, w_qkv, positions)
    appended = jnp.concatenate([new_keys.reshape(row_count, -1), new_values], axis=1)
    own_queries = queries.reshape(row_count, KV_HEADS, group_size, HEAD)
    cache_k, cache_v, span_all = (
        lax.all_gather(k_cache, "seq", axis=1, tiled=True),
        lax.all_gather(v_cache, "seq", axis=1, tiled=True),
        lax.all_gather(appended[None], "seq", axis=1, tiled=True),
    )

    def cache_visible(first_key, key_count):
        key_index = first_key + jnp.arange(key_count, dtype=jnp.int32)
        return jnp.broadcast_to((key_index < length)[None, :], (row_count, key_count))

    def span_visible(first_key, key_count):
        key_index = first_key + jnp.arange(key_count, dtype=jnp.int32)
        return key_index[None, :] <= query_index[:, None]

    carried = attend_keys(
        empty_state(row_count),
        own_queries,
        cache_k[0].reshape(-1, KV_HEADS, HEAD),
        cache_v[0].reshape(-1, KV_HEADS, HEAD),
        cache_visible,
    )
    carried = attend_keys(
        carried,
        own_queries,
        span_all[0][:, :key_width].reshape(-1, KV_HEADS, HEAD),
        span_all[0][:, key_width:].reshape(-1, KV_HEADS, HEAD),
        span_visible,
    )
    attended = finish_state(flatten_state(carried))
    stream = (
        tokens.astype(jnp.float32)
        + residual_scale * jnp.dot(attended, w_out, preferred_element_type=jnp.float32)
    ).astype(jnp.bfloat16)
    expert_in = rms_scale(stream, ffn_gain)
    top_count = routes.shape[1]
    route_rows = row_count * top_count
    slots_dev = expert_up.shape[0]
    req_count = lax.axis_size("req")
    device_count = req_count * seq_count
    slot_total = device_count * slots_dev
    capacity = 2 * ((row_count * top_count + slot_total - 1) // slot_total)
    slot_ids = jnp.take_along_axis(replica_slot, routes, axis=1).reshape(-1)
    slot_hot = (slot_ids[:, None] == jnp.arange(slot_total, dtype=jnp.int32)[None, :]).astype(
        jnp.bfloat16
    )
    route_order = jnp.arange(route_rows, dtype=jnp.int32)
    earlier = (route_order[:, None] > route_order[None, :]).astype(jnp.bfloat16)
    before = jnp.dot(earlier, slot_hot, preferred_element_type=jnp.float32)
    slot_rank = jnp.sum(before * slot_hot.astype(jnp.float32), axis=1).astype(jnp.int32)
    position = slot_ids * capacity + slot_rank
    place = jnp.any(
        (jnp.arange(slot_total * capacity, dtype=jnp.int32)[:, None] == position[None, :]).reshape(
            slot_total * capacity, row_count, top_count
        ),
        axis=2,
    ).astype(jnp.bfloat16)
    outgoing = jnp.dot(place, expert_in, preferred_element_type=jnp.float32).astype(jnp.bfloat16)
    outgoing = outgoing.reshape(device_count, slots_dev, capacity, -1)
    returned = lax.all_to_all(
        run_experts(
            lax.all_to_all(outgoing, ("req", "seq"), split_axis=0, concat_axis=0, tiled=True),
            expert_up,
            expert_down,
        ),
        ("req", "seq"),
        split_axis=0,
        concat_axis=0,
        tiled=True,
    )
    flat_back = returned.reshape(slot_total * capacity, -1)
    picked = flat_back[position].reshape(row_count, top_count, -1)
    shares = route_scores / jnp.sum(route_scores, axis=1, keepdims=True)
    expert_mix = jnp.sum(picked.astype(jnp.float32) * shares[:, :, None], axis=1).astype(
        jnp.bfloat16
    )
    return (attended, stream, expert_mix, appended)


def solution(mesh):
    return jax.shard_map(
        shards,
        mesh=mesh,
        in_specs=(
            P(("req", "seq"), None),
            P(),
            P(),
            P(),
            P("req", "seq", None),
            P("req", "seq", None),
            P("req"),
            P(),
            P(("req", "seq"), None),
            P(("req", "seq"), None),
            P(("req", "seq"), None),
            P(("req", "seq"), None, None),
            P(("req", "seq"), None, None),
        ),
        out_specs=(
            P(("req", "seq"), None),
            P(("req", "seq"), None),
            P(("req", "seq"), None),
            P(("req", "seq"), None),
        ),
        check_vma=False,
    )
```

profile of v0, /device:TPU:1, one launch (start us, length us, event | category | flops | bytes accessed | tf_op | source)
XLA Modules:
  0.0 339.3 jit_solution(17682309373478793448)
XLA Ops:
  8.7 1.2 fusion.46
  9.9 4.7 %fusion.54 = f32[128,2560]{1,0:T(8,128)S(1)} fusion(bf16[1536,2560]{1,0:T(8,128)(2,1)} %param.17, bf16[128,1536]{1,0:T(8,128)(2,1)} %param.15, f32[1536]{0:T(1024)} %param.16, f32[128]{0:T(128)S(1)} %add_rsqrt_fusion.1), kind=kOutput, calls=%fused_computation.81 | convolution fusion | flops 1007419392 | bytes 9574912 | tf_op jit(solution)/shard_map/dot_general | solution.py:44
  16.6 7.0 %gather_fusion.1 = s32[1024]{0:T(1024)S(1)} fusion(s32[128,40]{0,1:T(8,128)S(1)} %copy-done.1, s32[1024]{0:T(1024)S(1)} %reshape.286), kind=kCustom, calls=%fused_computation.1 | custom fusion | bytes 16384 | tf_op jit(solution)/shard_map/jit(take_along_axis)/gather | solution.py:207
  25.2 0.8 copy.106
  26.7 1.0 subtract_convert_fusion.1
  27.9 0.9 pad_maximum_fusion.1
  29.5 3.6 %all-gather = bf16[256,1024]{1,0:T(8,128)(2,1)} all-gather(bf16[128,1024]{1,0:T(8,128)(2,1)S(1)} %pad_maximum_fusion.1), channel_id=2, replica_groups=mesh['req'=64,'seq'=2] {'seq'}, dimensions={0}, use_global_device_ids=true | all-gather | bytes 786432 | tf_op jit(solution)/shard_map/all_gather | solution.py:169
  33.2 2.1 slice.49
  36.1 2.3 copy.102
  38.3 1.8 fusion.68
  40.2 2.1 reshape.310
  42.2 1.1 reshape.309
  43.3 1.2 subtract_convert_fusion
  45.3 8.1 %fusion.19 = pred[2048,128]{1,0:T(8,128)(4,1)} fusion(s32[128,8]{0,1:T(8,128)S(1)} %fusion.67), kind=kLoop, calls=%fused_computation.32 | loop fusion | flops 3932160 | bytes 266240 | tf_op jit(solution)/shard_map/reduce_or | solution.py:216
  53.4 0.8 broadcast_compare_fusion
  54.2 1.6 fusion.33
  55.9 1.7 copy-done.7
  57.6 1.8 convert_reduce_fusion.1
  59.4 6.2 %reshape.308 = bf16[2,8,128,8,64]{4,3,2,1,0:T(8,128)(2,1)} reshape(bf16[1,2048,512]{2,1,0:T(8,128)(2,1)} %all-gather.6.cloned.1.call-done) | data formatting | bytes 4194304 | tf_op jit(solution)/shard_map/reshape;reshape;squeeze | solution.py:89
  65.5 5.5 %copy.105 = bf16[2,8,128,8,64]{2,4,1,3,0:T(8,128)(2,1)} copy(bf16[2,8,128,8,64]{4,3,2,1,0:T(8,128)(2,1)} %reshape.308) | data formatting | bytes 4194304
  71.0 6.2 %reshape.307 = bf16[2,8,128,8,64]{4,3,2,1,0:T(8,128)(2,1)} reshape(bf16[1,2048,512]{2,1,0:T(8,128)(2,1)} %all-gather.4.cloned.1.call-done) | data formatting | bytes 4194304 | tf_op jit(solution)/shard_map/reshape;reshape;squeeze | solution.py:88
  77.2 5.5 %copy.104 = bf16[2,8,128,8,64]{2,4,1,3,0:T(8,128)(2,1)} copy(bf16[2,8,128,8,64]{4,3,2,1,0:T(8,128)(2,1)} %reshape.307) | data formatting | bytes 4194304
  83.2 32.9 %while.5 = (s32[]{:T(128)}, f32[128,8,3]{0,2,1:T(4,128)S(1)}, f32[128,8,3]{0,2,1:T(4,128)}, f32[128,8,3,64]{0,3,2,1:T(8,128)}, s32[2]{0:T(128)}, /*index=5*/s32[...) while((s32[]{:T(128)}, f32[128,8,3]{0,2,1:T(4,128)S(1)}, ...), condition=%wide.region_7.8_spmd.clone, body=%wide.region_1.7_spmd.clone.sunk | while | flops 856075264 | bytes 59203896 | solution.py:97
  83.7 1.3 dynamic_slice.46
  86.3 4.6 %fusion.81 = (f32[128,8,3,8]{0,2,3,1:T(4,128)S(1)}, f32[8,8,128,128,3]{3,2,4,1,0:T(8,128)S(1)}) fusion(pred[8,128]{1,0:T(8,128)(4,1)S(1)} %add_compare_fusion.2, bf16[128,8,3,64]{0,3,2,1:T(8,128)(2,1)S(1)} %get-tuple-element.378, bf16[2,8,128,8,64]{2,4,1,3,0:T(8,128)(2,1)} %get-tuple-element.377, s32[]{:T(128)S(6)} %copy.159), kind=kOutput, calls=%fused_computation.8.clone.1 | convolution fusion | flops 412065792 | bytes 14124036 | tf_op jit(solution)/shard_map/while/body/eval_jaxpr/rkgh,nbkh->rkgnb/dot_general | solution.py:59
  90.9 4.5 %convert_reduce_fusion.3 = (f32[128,8,3,8]{0,2,3,1:T(4,128)S(1)}, f32[128,8,3]{0,2,1:T(4,128)S(1)}) fusion(f32[128,8,3,8]{0,2,3,1:T(4,128)S(1)} %get-tuple-element.339, f32[8,8,128,128,3]{3,2,4,1,0:T(8,128)S(1)} %get-tuple-element.340, pred[8,128]{1,0:T(8,128)(4,1)S(1)} %add_compare_fusion.2), kind=kLoop, calls=%fused_computation.7.clone.1 | loop fusion | flops 25138176 | bytes 12792832 | tf_op jit(solution)/shard_map/while/body/eval_jaxpr/reduce_sum | solution.py:67
  95.5 3.2 fusion.83
  99.9 1.3 dynamic_slice.46
  102.5 4.6 %fusion.81 = (f32[128,8,3,8]{0,2,3,1:T(4,128)S(1)}, f32[8,8,128,128,3]{3,2,4,1,0:T(8,128)S(1)}) fusion(pred[8,128]{1,0:T(8,128)(4,1)S(1)} %add_compare_fusion.2, bf16[128,8,3,64]{0,3,2,1:T(8,128)(2,1)S(1)} %get-tuple-element.378, bf16[2,8,128,8,64]{2,4,1,3,0:T(8,128)(2,1)} %get-tuple-element.377, s32[]{:T(128)S(6)} %copy.159), kind=kOutput, calls=%fused_computation.8.clone.1 | convolution fusion | flops 412065792 | bytes 14124036 | tf_op jit(solution)/shard_map/while/body/eval_jaxpr/rkgh,nbkh->rkgnb/dot_general | solution.py:59
  107.1 4.5 %convert_reduce_fusion.3 = (f32[128,8,3,8]{0,2,3,1:T(4,128)S(1)}, f32[128,8,3]{0,2,1:T(4,128)S(1)}) fusion(f32[128,8,3,8]{0,2,3,1:T(4,128)S(1)} %get-tuple-element.339, f32[8,8,128,128,3]{3,2,4,1,0:T(8,128)S(1)} %get-tuple-element.340, pred[8,128]{1,0:T(8,128)(4,1)S(1)} %add_compare_fusion.2), kind=kLoop, calls=%fused_computation.7.clone.1 | loop fusion | flops 25138176 | bytes 12792832 | tf_op jit(solution)/shard_map/while/body/eval_jaxpr/reduce_sum | solution.py:67
  111.7 3.2 fusion.83
  116.8 0.8 multiply_reduce_fusion.1
  117.6 0.7 multiply_add_fusion.1
  118.4 3.0 fusion.40
  121.6 3.3 fusion.43
  125.0 1.9 convolution_convert_fusion
  126.8 85.9 %all_to_all.10 = bf16[128,1,16,1536]{3,2,1,0:T(8,128)(2,1)S(1)} all-to-all(bf16[128,1,16,1536]{3,2,1,0:T(8,128)(2,1)S(1)} %bitcast.147), channel_id=1, replica_groups=mesh['req'=64,'seq'=2] {'req','seq'}, dimensions={0} | all-to-all | bytes 12582912 | tf_op jit(solution)/shard_map/all_to_all | solution.py:226
  212.8 11.9 %fusion.26 = f32[128,1,16,1024]{3,0,2,1:T(8,128)S(1)} fusion(bf16[128,1,16,1536]{3,2,1,0:T(8,128)(2,1)S(1)} %all_to_all.10, bf16[1,1536,1024]{2,1,0:T(8,128)(2,1)S(1)} %copy-done), kind=kOutput, calls=%fused_computation.44 | convolution fusion | flops 6442450944 | bytes 17825792 | tf_op jit(solution)/shard_map/sjcd,jdf->sjcf/dot_general | solution.py:130
  224.7 4.0 %convert_bitcast_fusion = bf16[128,1,16,1536]{3,0,2,1:T(8,128)(2,1)S(1)} fusion(f32[128,1,16,1024]{3,0,2,1:T(8,128)S(1)} %fusion.26, bf16[1,512,1536]{2,1,0:T(8,128)(2,1)S(1)} %copy-done.24), kind=kOutput, calls=%fused_computation.39 | convolution fusion | flops 3230662656 | bytes 16252928 | tf_op jit(solution)/shard_map/sjcf,jfd->sjcd/dot_general | solution.py:135
  228.7 6.2 %copy.119 = bf16[128,1,16,1536]{3,2,1,0:T(8,128)(2,1)} copy(bf16[128,1,16,1536]{3,0,2,1:T(8,128)(2,1)S(1)} %convert_bitcast_fusion) | data formatting | bytes 12582912 | tf_op jit(solution)/shard_map/convert_element_type | solution.py:137
  234.8 5.6 %all-to-all-start.1 = ((bf16[128,1,16,1536]{3,2,1,0:T(8,128)(2,1)}), bf16[128,1,16,1536]{3,2,1,0:T(8,128)(2,1)}, u32[]{:S(2)}, u32[]{:S(2)}) async-start(bf16[128,1,16,1536]{3,2,1,0:T(8,128)(2,1)} %copy.119), calls=%async_computation.1 | async-start | bytes 12582912 | tf_op jit(solution)/shard_map/all_to_all | solution.py:224
  240.4 0.7 copy.120
  241.2 0.9 mul.312
  243.3 0.7 copy.121
  244.1 0.9 copy.122
  245.0 70.8 %all-to-all-done.1 = bf16[128,1,16,1536]{3,2,1,0:T(8,128)(2,1)} async-done(((bf16[128,1,16,1536]{3,2,1,0:T(8,128)(2,1)}), bf16[128,1,16,1536]{3,2,1,0:T(8,128)(2,1)}, u32[]{:S(2)}, u32[]{:S(2)}) %all-to-all-start.1) | async-done | bytes 6291488 | tf_op jit(solution)/shard_map/all_to_all | solution.py:224
  315.8 10.9 %gather_fusion = bf16[1024,1536]{1,0:T(8,128)(2,1)} fusion(bf16[2048,1536]{1,0:T(8,128)(2,1)} %bitcast.31, s32[1024]{0:T(1024)S(1)} %broadcast_clamp_fusion), kind=kCustom, calls=%fused_computation | custom fusion | bytes 6295552 | tf_op jit(solution)/shard_map/gather | solution.py:236
  326.7 5.5 %fusion.20 = bf16[128,1536]{1,0:T(8,128)(2,1)} fusion(bf16[1024,1536]{1,0:T(8,128)(2,1)} %gather_fusion, f32[128,8]{1,0:T(8,128)S(1)} %copy-done.14), kind=kLoop, calls=%fused_computation.35 | loop fusion | flops 4521984 | bytes 3543040 | tf_op jit(solution)/shard_map/reduce_sum | solution.py:238
  (113 shorter events, 14.1 us)
Async XLA Ops:
  7.2 205.6 %copy-start = (bf16[1,1536,1024]{2,1,0:T(8,128)(2,1)S(1)}, bf16[1,1536,1024]{2,1,0:T(8,128)(2,1)}, u32[]{:S(2)}) copy-start(bf16[1,1536,1024]{2,1,0:T(8,128)(2,1)} %param.26) | copy-start | bytes 9437188
  7.2 52.2 %all-gather.6.cloned.1.call-start = ((), (), s32[]{:S(2)}) async-start(), calls=%async_computation.3 | async-start | bytes 3145728 | tf_op jit(solution)/shard_map/all_gather | solution.py:168
  7.9 63.1 %all-gather.4.cloned.1.call-start = ((), (), s32[]{:S(2)}) async-start(), calls=%async_computation.2 | async-start | bytes 3145728 | tf_op jit(solution)/shard_map/all_gather | solution.py:167
  9.8 6.5 %copy-start.22 = (s32[128,8]{0,1:T(8,128)S(1)}, s32[128,8]{0,1:T(8,128)}, u32[]{:S(2)}) copy-start(s32[128,8]{0,1:T(8,128)} %param.23) | copy-start | bytes 12292
  14.5 1.1 copy-start.6
  14.6 2.0 copy-start.1
  24.3 3.4 %copy-start.19 = (s32[128,8]{0,1:T(8,128)}, s32[128,8]{0,1:T(8,128)S(1)}, u32[]{:S(2)}) copy-start(s32[128,8]{0,1:T(8,128)S(1)} %get-tuple-element.255) | copy-start | bytes 12292
  28.8 0.7 copy-start.11
  35.3 9.2 %copy-start.17 = (s32[1024]{0:T(1024)}, s32[1024]{0:T(1024)S(1)}, u32[]{:S(2)}) copy-start(s32[1024]{0:T(1024)S(1)} %convert_element_type.121) | copy-start | bytes 12292
  54.2 1.7 copy-start.15
  55.9 1.7 copy-start.7
  55.9 1.7 copy-start.16
  90.9 4.6 %copy-start.8 = (bf16[2,8,128,8,64]{2,4,1,3,0:T(8,128)(2,1)S(1)}, bf16[2,8,128,8,64]{2,4,1,3,0:T(8,128)(2,1)}, u32[]{:S(2)}) copy-start(bf16[2,8,128,8,64]{2,4,1,3,0:T(8,128)(2,1)} %get-tuple-element.379) | copy-start | bytes 6291460 | tf_op jit(solution)/shard_map/while
  95.5 3.2 copy-start.12
  95.5 3.2 copy-start.2
  98.7 0.6 copy-start.13
  99.0 0.9 copy-start.3
  107.1 4.6 %copy-start.8 = (bf16[2,8,128,8,64]{2,4,1,3,0:T(8,128)(2,1)S(1)}, bf16[2,8,128,8,64]{2,4,1,3,0:T(8,128)(2,1)}, u32[]{:S(2)}) copy-start(bf16[2,8,128,8,64]{2,4,1,3,0:T(8,128)(2,1)} %get-tuple-element.379) | copy-start | bytes 6291460 | tf_op jit(solution)/shard_map/while
  111.7 3.2 copy-start.12
  111.7 3.2 copy-start.2
  114.9 0.6 copy-start.13
  115.2 0.9 copy-start.3
  118.4 3.0 copy-start.4
  118.4 3.2 copy-start.5
  121.4 3.6 %copy-start.9 = (pred[2048,128]{1,0:T(8,128)(4,1)S(1)}, pred[2048,128]{1,0:T(8,128)(4,1)}, u32[]{:S(2)}) copy-start(pred[2048,128]{1,0:T(8,128)(4,1)} %fusion.19) | copy-start | bytes 786436
  121.4 3.6 %copy-start.23 = (f32[1536]{0:T(1024)S(1)}, f32[1536]{0:T(1024)}, u32[]{:S(2)}) copy-start(f32[1536]{0:T(1024)} %param.22) | copy-start | bytes 18436
  124.9 1.9 copy-start.10
  212.8 11.9 %copy-start.24 = (bf16[1,512,1536]{2,1,0:T(8,128)(2,1)S(1)}, bf16[1,512,1536]{2,1,0:T(8,128)(2,1)}, u32[]{:S(2)}) copy-start(bf16[1,512,1536]{2,1,0:T(8,128)(2,1)} %param.27) | copy-start | bytes 4718596
  234.8 5.6 %copy-start.21 = (s32[128,8]{0,1:T(8,128)S(1)}, s32[128,8]{0,1:T(8,128)}, u32[]{:S(2)}) copy-start(s32[128,8]{0,1:T(8,128)} %get-tuple-element.254) | copy-start | bytes 12292
  234.8 7.3 %copy-start.20 = (f32[128,8]{0,1:T(8,128)S(1)}, f32[128,8]{0,1:T(8,128)}, u32[]{:S(2)}) copy-start(f32[128,8]{0,1:T(8,128)} %param.24) | copy-start | bytes 12292
  234.8 9.2 %copy-start.18 = (s32[1024]{0:T(1024)S(1)}, s32[1024]{0:T(1024)}, u32[]{:S(2)}) copy-start(s32[1024]{0:T(1024)} %copy-done.17) | copy-start | bytes 12292
  234.8 81.0 %all-to-all-start.1 = ((bf16[128,1,16,1536]{3,2,1,0:T(8,128)(2,1)}), bf16[128,1,16,1536]{3,2,1,0:T(8,128)(2,1)}, u32[]{:S(2)}, u32[]{:S(2)}) async-start(bf16[128,1,16,1536]{3,2,1,0:T(8,128)(2,1)} %copy.119), calls=%async_computation.1 | async-start | bytes 12582912 | tf_op jit(solution)/shard_map/all_to_all | solution.py:224
  315.8 11.0 %copy-start.14 = (f32[128,8]{1,0:T(8,128)S(1)}, f32[128,8]{1,0:T(8,128)}, u32[]{:S(2)}) copy-start(f32[128,8]{1,0:T(8,128)} %copy.121) | copy-start | bytes 12292
Sparse Core Ops, SparseCore 0:
  9.7 16.9 all-gather.5
  28.3 14.6 all-gather.3
where the time goes:
time: 343 us; the launch traced here: 339 us
  blocking collectives  89.6 us (26%)
  waiting for transfers between devices  72.2 us (21%)
  local copies, waits for them, and re-layouts  70.8 us (21%)
  matrix products  46.4 us (14%)
  other arithmetic  37.4 us (11%)
  between operations  15.3 us (4%)
  starting transfers between devices  5.67 us (2%)
    all_to_all x1, blocking collectives, shards(): lax.all_to_all(outgoing, ('req', 'seq'), split_axis=0, concat_axis=0, til...  85.9 us
    all_to_all x1, waiting for transfers between devices, shards(): lax.all_to_all(run_experts(lax.all_to_all(outgoing, ('req', 'seq'), split...  70.8 us
    unnamed x43, local copies, waits for them, and re-layouts  14.8 us
    dot_general x1, matrix products, run_experts(): jnp.einsum('sjcd,jdf->sjcf', buffer, expert_up, preferred_element_type=jn...  11.9 us
    gather x1, local copies, waits for them, and re-layouts, shards(): picked = flat_back[position].reshape(row_count, top_count, -1)  10.9 us
    dot_general x3, matrix products, fold_blocks(): jnp.einsum('rkgh,nbkh->rkgnb', queries, key_part, preferred_element_type=...  10.8 us
    reduce_sum x3, other arithmetic, fold_blocks(): totals = jnp.sum(weights, axis=-1, dtype=jnp.float32)  10.7 us
    dot_general x3, matrix products, fold_blocks(): jnp.einsum('rkgnb,nbkh->rkgnh', weights, value_part, preferred_element_ty...  9.27 us
  transfers between devices with their start and end apart: 3, of which 1 were waited for; matrix products, arithmetic and copies ran while one was open for 18% of the time, Pallas kernels for 0%

commit v1 on v0

v1 whole, which is shorter than its diff:
```python
import functools
import numpy as np
import jax
import jax.numpy as jnp
from jax import lax
from jax.experimental import pallas as pl
from jax.experimental.pallas import tpu as pltpu
from jax.sharding import PartitionSpec as P

HEADS = 24
KV_HEADS = 8
HEAD = 64
CAP = 16
MESH = pl.DeviceIdType.MESH

epsilon = 1e-06
residual_scale = 0.22
score_scale = 0.015625
rope_base = 10000.0
neg_big = -1e30


def norm_rows(rows, gain):
    widened = rows.astype(jnp.float32)
    mean_square = jnp.mean(widened * widened, axis=-1, keepdims=True)
    return (widened * lax.rsqrt(mean_square + epsilon) * gain).astype(jnp.bfloat16)


def attention_kernel(
    length_ref, tokens_ref, attn_gain_ref, ffn_gain_ref, freq_ref, routes_ref, scores_ref, replica_ref,
    w_qkv_ref, w_out_ref, k_cache_ref, v_cache_ref,
    attended_ref, stream_ref, expert_in_ref, appended_ref, meta_ref,
    w_qkv, w_out, keys, values, queries, heads_out, weight_sems, cache_sems, send_sems, recv_sems,
):
    rows, width = tokens_ref.shape
    cache_half = k_cache_ref.shape[0]
    kv_width = KV_HEADS * HEAD
    q_width = HEADS * HEAD
    group = HEADS // KV_HEADS
    req, me = lax.axis_index("req"), lax.axis_index("seq")
    partner = 1 - me

    qkv_chunk = 512
    order = (3, 4, 0, 1, 2)
    weight_copies = []
    for at in order:
        cols = pl.ds(at * qkv_chunk, qkv_chunk)
        copy = pltpu.make_async_copy(w_qkv_ref.at[:, cols], w_qkv.at[:, cols], weight_sems.at[at])
        copy.start()
        weight_copies.append(copy)
    mine = pl.ds(pl.multiple_of(me * cache_half, cache_half), cache_half)
    local_k = pltpu.make_async_copy(k_cache_ref, keys.at[mine], cache_sems.at[0])
    local_v = pltpu.make_async_copy(v_cache_ref, values.at[mine], cache_sems.at[1])
    local_k.start()
    local_v.start()
    out_copy = pltpu.make_async_copy(w_out_ref, w_out, weight_sems.at[5])
    out_copy.start()

    barrier = pltpu.get_barrier_semaphore()
    pl.semaphore_signal(barrier, inc=1, device_id=(req, partner), device_id_type=MESH)
    pl.semaphore_wait(barrier, 1)

    def to_partner(src, dst, at):
        return pltpu.make_async_remote_copy(
            src_ref=src, dst_ref=dst, send_sem=send_sems.at[at], recv_sem=recv_sems.at[at],
            device_id=(req, partner), device_id_type=MESH,
        )

    send_k = to_partner(k_cache_ref, keys.at[mine], 0)
    send_v = to_partner(v_cache_ref, values.at[mine], 1)
    send_k.start()
    send_v.start()

    top = routes_ref.shape[1]
    lanes = lax.broadcasted_iota(jnp.int32, (rows, 128), 1)
    row_ids = lax.broadcasted_iota(jnp.int32, (rows, 128), 0)
    experts = replica_ref.shape[1]
    expert_lane = lax.broadcasted_iota(jnp.int32, (rows, experts), 1)
    replica = replica_ref[...].astype(jnp.float32)
    routes = routes_ref[...]
    slots = []
    hits = jnp.zeros((rows, 128), jnp.float32)
    for k in range(top):
        slot = jnp.sum(jnp.where(expert_lane == routes[:, k : k + 1], replica, 0.0), axis=1, keepdims=True)
        slots.append(slot)
        hits = hits + jnp.where(lanes == slot.astype(jnp.int32), 1.0, 0.0)
    earlier = jnp.where(row_ids > lanes, 1.0, 0.0).astype(jnp.bfloat16)
    before = jnp.dot(earlier, hits.astype(jnp.bfloat16), preferred_element_type=jnp.float32)
    scores = scores_ref[...]
    shares = scores / jnp.sum(scores, axis=1, keepdims=True)
    table = jnp.zeros((rows, 128), jnp.float32)
    for k in range(top):
        rank = jnp.sum(jnp.where(lanes == slots[k].astype(jnp.int32), before, 0.0), axis=1, keepdims=True)
        table = jnp.where(lanes == k, slots[k], table)
        table = jnp.where(lanes == top + k, rank, table)
        table = jnp.where(lanes == 2 * top + k, shares[:, k : k + 1], table)
    meta_ref[...] = jnp.transpose(table)[: meta_ref.shape[0], :].astype(meta_ref.dtype)

    normed = norm_rows(tokens_ref[...], attn_gain_ref[...])
    length = length_ref[0]
    positions = (length + me * rows + row_ids).astype(jnp.float32)
    angles = positions * freq_ref[...]
    cosine = jnp.cos(angles)
    sine = jnp.sin(angles)
    lower = (lanes % HEAD) < HEAD // 2
    signed_sine = jnp.where(lower, -sine, sine)

    def rotated(tile):
        swapped = jnp.where(lower, pltpu.roll(tile, 128 - HEAD // 2, 1), pltpu.roll(tile, HEAD // 2, 1))
        return (tile * cosine + swapped * signed_sine).astype(jnp.bfloat16)

    own_span = pl.ds(pl.multiple_of(2 * cache_half + me * rows, rows), rows)
    even_half = lanes < HEAD
    for turn, at in enumerate(order):
        weight_copies[turn].wait()
        projected = jnp.dot(
            normed, w_qkv[:, at * qkv_chunk : (at + 1) * qkv_chunk], preferred_element_type=jnp.float32
        )
        if at == 3:
            for tile in range(qkv_chunk // 128):
                new_keys = rotated(projected[:, tile * 128 : (tile + 1) * 128])
                keys[own_span, tile * 128 : (tile + 1) * 128] = new_keys
                appended_ref[:, tile * 128 : (tile + 1) * 128] = new_keys
            send_new_k = to_partner(keys.at[own_span], keys.at[own_span], 2)
            send_new_k.start()
        elif at == 4:
            new_values = projected.astype(jnp.bfloat16)
            values[own_span, :] = new_values
            appended_ref[:, kv_width:] = new_values
            send_new_v = to_partner(values.at[own_span], values.at[own_span], 3)
            send_new_v.start()
        else:
            for tile in range(qkv_chunk // 128):
                turned = rotated(projected[:, tile * 128 : (tile + 1) * 128]).astype(jnp.float32) * score_scale
                other = pltpu.roll(turned, HEAD, 1)
                for half in range(2):
                    head = (at * qkv_chunk // 128 + tile) * 2 + half
                    kv, member = head // group, head % group
                    source = turned if half == kv % 2 else other
                    keep = even_half if kv % 2 == 0 else jnp.logical_not(even_half)
                    queries[kv, member * rows : (member + 1) * rows, :] = jnp.where(keep, source, 0.0).astype(jnp.bfloat16)

    local_k.wait()
    local_v.wait()
    send_k.wait()
    send_v.wait()
    send_new_k.wait()
    send_new_v.wait()
    key_total = 2 * cache_half + 2 * rows
    key_lane = lax.broadcasted_iota(jnp.int32, (1, 2 * cache_half), 1)
    cache_bias = jnp.where(key_lane < length, 0.0, neg_big)
    span_lane = lax.broadcasted_iota(jnp.int32, (rows, 2 * rows), 1)
    span_row = lax.broadcasted_iota(jnp.int32, (rows, 2 * rows), 0) + me * rows
    span_bias = jnp.where(span_lane <= span_row, 0.0, neg_big)
    ones = jnp.ones((key_total, 128), jnp.bfloat16)
    dims = (((1,), (1,)), ((), ()))

    def one_group(kv, _):
        pair = pl.ds(pl.multiple_of((kv // 2) * 128, 128), 128)
        pair_keys = keys[:, pair]
        pair_values = jnp.concatenate([values[:, pair], ones], axis=1)
        for member in range(group):
            q = queries[kv, member * rows : (member + 1) * rows, :]
            s_cache = lax.dot_general(q, pair_keys[: 2 * cache_half], dims, preferred_element_type=jnp.float32) + cache_bias
            s_span = lax.dot_general(q, pair_keys[2 * cache_half :], dims, preferred_element_type=jnp.float32) + span_bias
            best = jnp.maximum(jnp.max(s_cache, axis=1, keepdims=True), jnp.max(s_span, axis=1, keepdims=True))
            w_cache = jnp.exp(s_cache - best).astype(jnp.bfloat16)
            w_span = jnp.exp(s_span - best).astype(jnp.bfloat16)
            summed = jnp.dot(w_cache, pair_values[: 2 * cache_half], preferred_element_type=jnp.float32)
            summed = summed + jnp.dot(w_span, pair_values[2 * cache_half :], preferred_element_type=jnp.float32)
            heads_out[kv, member * rows : (member + 1) * rows, :] = summed[:, :128] / summed[:, 128:]
        return 0

    lax.fori_loop(0, KV_HEADS, one_group, 0)

    for tile in range(q_width // 128):
        parts = []
        for half in range(2):
            head = tile * 2 + half
            kv, member = head // group, head % group
            part = heads_out[kv, member * rows : (member + 1) * rows, :]
            parts.append(part if half == kv % 2 else pltpu.roll(part, HEAD, 1))
        attended_ref[:, tile * 128 : (tile + 1) * 128] = jnp.where(even_half, parts[0], parts[1]).astype(jnp.bfloat16)

    out_copy.wait()
    attended = attended_ref[...]
    chunk = 512
    for at in range(width // chunk):
        cols = slice(at * chunk, (at + 1) * chunk)
        product = jnp.dot(attended, w_out[:, cols], preferred_element_type=jnp.float32)
        stream_ref[:, cols] = (tokens_ref[:, cols].astype(jnp.float32) + residual_scale * product).astype(jnp.bfloat16)
    expert_in_ref[...] = norm_rows(stream_ref[...], ffn_gain_ref[...])


def attention_call(tokens, attn_gain, w_qkv, w_out, k_cache, v_cache, cache_len, ffn_gain, routes, route_scores, replica_slot):
    rows, width = tokens.shape
    cache_half = k_cache.shape[1]
    kv_width = KV_HEADS * HEAD
    key_total = 2 * cache_half + 2 * rows
    half = HEAD // 2
    freq = np.float64(rope_base) ** (-(np.arange(128) % half) / half)
    freq = jnp.asarray(freq[None, :], jnp.float32)
    vmem = pl.BlockSpec(memory_space=pltpu.VMEM)
    hbm = pl.BlockSpec(memory_space=pl.ANY)
    shape = lambda *dims: jax.ShapeDtypeStruct(dims, jnp.bfloat16)
    return pl.pallas_call(
        attention_kernel,
        name="attention",
        out_shape=(shape(rows, width), shape(rows, width), shape(rows, width), shape(rows, 2 * kv_width), shape(32, 128)),
        in_specs=[pl.BlockSpec(memory_space=pltpu.SMEM)] + [vmem] * 7 + [hbm] * 4,
        out_specs=(vmem,) * 5,
        scratch_shapes=[
            pltpu.VMEM(w_qkv.shape, jnp.bfloat16),
            pltpu.VMEM(w_out.shape, jnp.bfloat16),
            pltpu.VMEM((key_total, kv_width), jnp.bfloat16),
            pltpu.VMEM((key_total, kv_width), jnp.bfloat16),
            pltpu.VMEM((KV_HEADS, HEADS // KV_HEADS * rows, 128), jnp.bfloat16),
            pltpu.VMEM((KV_HEADS, HEADS // KV_HEADS * rows, 128), jnp.float32),
            pltpu.SemaphoreType.DMA((6,)),
            pltpu.SemaphoreType.DMA((2,)),
            pltpu.SemaphoreType.DMA((4,)),
            pltpu.SemaphoreType.DMA((4,)),
        ],
        compiler_params=pltpu.CompilerParams(
            collective_id=0, has_side_effects=True, vmem_limit_bytes=60 * 1024 * 1024
        ),
    )(cache_len, tokens, attn_gain[None], ffn_gain[None], freq, routes, route_scores, replica_slot,
      w_qkv, w_out, k_cache[0], v_cache[0])


def run_experts(buffer, expert_up, expert_down):
    gate_up = jnp.einsum("sjcd,jdf->sjcf", buffer, expert_up, preferred_element_type=jnp.float32)
    hidden_width = expert_down.shape[1]
    active = (jax.nn.silu(gate_up[..., :hidden_width]) * gate_up[..., hidden_width:]).astype(
        jnp.bfloat16
    )
    return jnp.einsum(
        "sjcf,jfd->sjcd", active, expert_down, preferred_element_type=jnp.float32
    ).astype(jnp.bfloat16)


def shards(tokens, attn_gain, w_qkv, w_out, k_cache, v_cache, cache_len, ffn_gain, routes, route_scores, replica_slot, expert_up, expert_down):
    rows, width = tokens.shape
    attended, stream, expert_in, appended, meta = attention_call(
        tokens, attn_gain, w_qkv, w_out, k_cache, v_cache, cache_len, ffn_gain, routes, route_scores, replica_slot
    )
    top = routes.shape[1]
    slot_total = lax.axis_size("req") * lax.axis_size("seq")
    wide = meta.astype(jnp.float32)
    position = wide[:top] * CAP + wide[top : 2 * top]
    share = wide[2 * top : 3 * top]
    place_ids = jnp.arange(slot_total * CAP, dtype=jnp.float32)
    mix = jnp.sum(jnp.where(place_ids[None, :, None] == position[:, None, :], share[:, None, :], 0.0), axis=0)
    place = (mix > 0).astype(jnp.bfloat16)
    mix = mix.astype(jnp.bfloat16)
    outgoing = jnp.dot(place, expert_in, preferred_element_type=jnp.float32).astype(jnp.bfloat16)
    outgoing = outgoing.reshape(slot_total, 1, CAP, width)
    exchange = functools.partial(lax.all_to_all, axis_name=("req", "seq"), split_axis=0, concat_axis=0, tiled=True)
    returned = exchange(run_experts(exchange(outgoing), expert_up, expert_down)).reshape(slot_total * CAP, width)
    expert_mix = lax.dot_general(mix, returned, (((0,), (0,)), ((), ())), preferred_element_type=jnp.float32).astype(jnp.bfloat16)
    return (attended, stream, expert_mix, appended)


def solution(mesh):
    rows2 = P(("req", "seq"), None)
    rows3 = P(("req", "seq"), None, None)
    cache = P("req", "seq", None)
    return jax.shard_map(
        shards,
        mesh=mesh,
        in_specs=(rows2, P(), P(), P(), cache, cache, P("req"), P(), rows2, rows2, rows2, rows3, rows3),
        out_specs=(rows2,) * 4,
        check_vma=False,
    )
```

time: 343 us -> 233 us (0.68)
  local copies, waits for them, and re-layouts: 70.8 us -> 16.1 us
  other arithmetic: 37.4 us -> 1.86 us
  matrix products: 46.4 us -> 23.8 us
  Pallas kernels: 0 us -> 22.1 us
  between operations: 15.3 us -> 1.51 us
    dot_general x9 -> x1, matrix products: 28.6 us -> 4.93 us  [shards(): lax.dot_general(mix, returned, (((0,), (0,)), ((), ())), preferred_elemen...]
    pallas_call x0 -> x1, Pallas kernels: none -> 22.1 us  [attention_call(): pl.pallas_call(attention_kernel, name='attention', out_shape=(shape(rows,...]
    gather x6 -> x0, local copies, waits for them, and re-layouts: 18.3 us -> none  [the longest x1 10.9 us: shards(): picked = flat_back[position].reshape(row_count, top_count, -1)]
    reduce_sum x9 -> x1, other arithmetic: 18.8 us -> 1.16 us  [shards(): jnp.sum(jnp.where(place_ids[None, :, None] == position[:, None, :], share...]
    another operation x2 -> x0, local copies, waits for them, and re-layouts: 12.3 us -> none  [the longest x1 6.15 us: attend_keys(): value_rows.reshape(turn_count, group_size, KEY_BLOCK, KV_HEADS, HEAD)]
    unnamed x43 -> x18, local copies, waits for them, and re-layouts: 14.8 us -> 6.51 us
    reduce_or x1 -> x0, other arithmetic: 8.11 us -> none  [shards(): jnp.any((jnp.arange(slot_total * capacity, dtype=jnp.int32)[:, None] == p...]
    slice x6 -> x1, local copies, waits for them, and re-layouts: 7.74 us -> 0.67 us  [shards(): share = wide[2 * top:3 * top]]
  transfers between devices with their start and end apart: 3 -> 1, of which waited for: 1 -> 1; matrix products, arithmetic and copies ran while one was open for 18% -> 0% of each run, Pallas kernels for 0% -> 0%
where the time goes in v1:
time: 233 us; the launch traced here: 232 us
  blocking collectives  86.2 us (37%)
  waiting for transfers between devices  75.4 us (32%)
  matrix products  23.8 us (10%)
  Pallas kernels  22.1 us (9%)
  local copies, waits for them, and re-layouts  16.1 us (7%)
  starting transfers between devices  5.48 us (2%)
    all_to_all x1, blocking collectives, shards(): exchange(outgoing)  86.2 us
    all_to_all x1, waiting for transfers between devices, shards(): exchange(run_experts(exchange(outgoing), expert_up, expert_down))  75.4 us
    pallas_call x1, Pallas kernels, attention_call(): pl.pallas_call(attention_kernel, name='attention', out_shape=(shape(rows,...  22.1 us
    dot_general x1, matrix products, run_experts(): jnp.einsum('sjcd,jdf->sjcf', buffer, expert_up, preferred_element_type=jn...  11.8 us
    unnamed x18, local copies, waits for them, and re-layouts  6.51 us
    convert_element_type x1, local copies, waits for them, and re-layouts, run_experts(): return jnp.einsum('sjcf,jfd->sjcd', active, expert_down, preferred_elemen...  6.13 us
    all_to_all x1, starting transfers between devices, shards(): exchange(run_experts(exchange(outgoing), expert_up, expert_down))  5.48 us
    dot_general x1, matrix products, shards(): lax.dot_general(mix, returned, (((0,), (0,)), ((), ())), preferred_elemen...  4.93 us
  transfers between devices with their start and end apart: 1, of which 1 were waited for; matrix products, arithmetic and copies ran while one was open for 0% of the time, Pallas kernels for 0%

profile of v1, /device:TPU:1, one launch (start us, length us, event | category | flops | bytes accessed | tf_op | source)
XLA Modules:
  0.0 232.3 jit_solution(6671677040965786847)
XLA Ops:
  0.6 0.0 copy-start
  1.4 1.5 broadcast_in_dim.21.attn_gain_ref
  2.9 1.3 broadcast_in_dim.22.ffn_gain_ref
  4.2 1.4 copy.33.routes_ref
  5.6 1.4 copy.34.scores_ref
  7.0 1.5 copy.35.replica_ref
  8.5 22.1 %attention.1 = (bf16[128,1536]{1,0:T(8,128)(2,1)}, bf16[128,1536]{1,0:T(8,128)(2,1)}, bf16[128,1536]{1,0:T(8,128)(2,1)}, bf16[128,1024]{1,0:T(8,128)(2,1)}, bf16[32,128]{1,0:T(8,128)(2,1)}) custom-call(s32[1]{0:T(128)S(6)} %copy.48.length_ref, bf16[128,1536]{1,0:T(8,128)(2,1)} %tokens_ref.1, f32[1,1536]{1,0:T(1,128)} %broadcast_in_dim.21.attn_gain_ref, ...), custom_call_target="tpu_custom_call" | custom-call | tf_op jit(solution)/shard_map/attention/pallas_call | solution.py:206
  30.6 0.7 slice.22
  31.2 0.7 convert_element_type.28
  31.9 1.2 select_reduce_fusion
  33.1 0.0 copy-start.1
  33.1 3.1 %convolution_convert_fusion = bf16[2048,1536]{1,0:T(8,128)(2,1)S(1)} fusion(bf16[128,1536]{1,0:T(8,128)(2,1)} %get-tuple-element.12, f32[2048,128]{1,0:T(8,128)S(1)} %select_reduce_fusion), kind=kOutput, calls=%fused_computation.2 | convolution fusion | flops 808714240 | bytes 7733248 | tf_op jit(solution)/shard_map/dot_general | solution.py:256
  36.2 86.2 %all_to_all.10 = bf16[128,1,16,1536]{3,2,1,0:T(8,128)(2,1)S(1)} all-to-all(bf16[128,1,16,1536]{3,2,1,0:T(8,128)(2,1)S(1)} %bitcast.36), channel_id=1, replica_groups=mesh['req'=64,'seq'=2] {'req','seq'}, dimensions={0} | all-to-all | bytes 12582912 | tf_op jit(solution)/shard_map/all_to_all | solution.py:259
  122.3 0.0 copy-done.1
  122.3 0.0 copy-done
  122.3 0.0 copy-start.5
  122.3 11.8 %fusion.4 = f32[128,1,16,1024]{3,0,2,1:T(8,128)S(1)} fusion(bf16[128,1,16,1536]{3,2,1,0:T(8,128)(2,1)S(1)} %all_to_all.10, bf16[1,1536,1024]{2,1,0:T(8,128)(2,1)S(1)} %copy-done), kind=kOutput, calls=%fused_computation.9 | convolution fusion | flops 6442450944 | bytes 17825792 | tf_op jit(solution)/shard_map/sjcd,jdf->sjcf/dot_general | solution.py:232
  134.2 0.0 copy-done.5
  134.2 4.0 %convert_bitcast_fusion = bf16[128,1,16,1536]{3,0,2,1:T(8,128)(2,1)S(1)} fusion(f32[128,1,16,1024]{3,0,2,1:T(8,128)S(1)} %fusion.4, bf16[1,512,1536]{2,1,0:T(8,128)(2,1)S(1)} %copy-done.5), kind=kOutput, calls=%fused_computation.6 | convolution fusion | flops 3230662656 | bytes 16252928 | tf_op jit(solution)/shard_map/sjcf,jfd->sjcd/dot_general | solution.py:237
  138.2 6.1 %copy.38 = bf16[128,1,16,1536]{3,2,1,0:T(8,128)(2,1)} copy(bf16[128,1,16,1536]{3,0,2,1:T(8,128)(2,1)S(1)} %convert_bitcast_fusion) | data formatting | bytes 12582912 | tf_op jit(solution)/shard_map/convert_element_type | solution.py:239
  144.3 5.5 %all-to-all-start.1 = ((bf16[128,1,16,1536]{3,2,1,0:T(8,128)(2,1)}), bf16[128,1,16,1536]{3,2,1,0:T(8,128)(2,1)}, u32[]{:S(2)}, u32[]{:S(2)}) async-start(bf16[128,1,16,1536]{3,2,1,0:T(8,128)(2,1)} %copy.38), calls=%async_computation.1 | async-start | bytes 12582912 | tf_op jit(solution)/shard_map/all_to_all | solution.py:259
  149.8 0.0 copy-start.2
  149.8 75.4 %all-to-all-done.1 = bf16[128,1,16,1536]{3,2,1,0:T(8,128)(2,1)} async-done(((bf16[128,1,16,1536]{3,2,1,0:T(8,128)(2,1)}), bf16[128,1,16,1536]{3,2,1,0:T(8,128)(2,1)}, u32[]{:S(2)}, u32[]{:S(2)}) %all-to-all-start.1) | async-done | bytes 6291488 | tf_op jit(solution)/shard_map/all_to_all | solution.py:259
  225.2 0.0 copy-start.3
  225.2 0.0 copy-start.4
  225.2 4.9 %convolution_convert_fusion.1 = bf16[128,1536]{1,0:T(8,128)(2,1)} fusion(bf16[2048,1536]{1,0:T(8,128)(2,1)} %bitcast.18, f32[2048,128]{1,0:T(8,128)} %copy-done.1), kind=kOutput, calls=%fused_computation.11 | convolution fusion | flops 805765120 | bytes 7733248 | tf_op jit(solution)/shard_map/dot_general | solution.py:260
  230.1 0.0 copy-done.3
  230.1 0.7 copy.49
  230.9 0.0 copy-done.2
  230.9 0.7 copy.50
  231.6 0.0 copy-done.4
  231.6 0.7 copy.51
  (1 shorter events, 0.0 us)
Async XLA Ops:
  0.6 121.7 %copy-start = (bf16[1,1536,1024]{2,1,0:T(8,128)(2,1)S(1)}, bf16[1,1536,1024]{2,1,0:T(8,128)(2,1)}, u32[]{:S(2)}) copy-start(bf16[1,1536,1024]{2,1,0:T(8,128)(2,1)} %param.25) | copy-start | bytes 9437188
  33.1 89.2 %copy-start.1 = (f32[2048,128]{1,0:T(8,128)}, f32[2048,128]{1,0:T(8,128)S(1)}, u32[]{:S(2)}) copy-start(f32[2048,128]{1,0:T(8,128)S(1)} %select_reduce_fusion) | copy-start | bytes 3145732
  122.3 11.9 %copy-start.5 = (bf16[1,512,1536]{2,1,0:T(8,128)(2,1)S(1)}, bf16[1,512,1536]{2,1,0:T(8,128)(2,1)}, u32[]{:S(2)}) copy-start(bf16[1,512,1536]{2,1,0:T(8,128)(2,1)} %param.26) | copy-start | bytes 4718596
  144.3 80.9 %all-to-all-start.1 = ((bf16[128,1,16,1536]{3,2,1,0:T(8,128)(2,1)}), bf16[128,1,16,1536]{3,2,1,0:T(8,128)(2,1)}, u32[]{:S(2)}, u32[]{:S(2)}) async-start(bf16[128,1,16,1536]{3,2,1,0:T(8,128)(2,1)} %copy.38), calls=%async_computation.1 | async-start | bytes 12582912 | tf_op jit(solution)/shard_map/all_to_all | solution.py:259
  149.8 81.0 %copy-start.2 = (bf16[128,1536]{1,0:T(8,128)(2,1)S(1)}, bf16[128,1536]{1,0:T(8,128)(2,1)}, u32[]{:S(2)}) copy-start(bf16[128,1536]{1,0:T(8,128)(2,1)} %get-tuple-element.19) | copy-start | bytes 1179652
  225.2 4.9 %copy-start.3 = (bf16[128,1536]{1,0:T(8,128)(2,1)S(1)}, bf16[128,1536]{1,0:T(8,128)(2,1)}, u32[]{:S(2)}) copy-start(bf16[128,1536]{1,0:T(8,128)(2,1)} %get-tuple-element.18) | copy-start | bytes 1179652
  225.2 6.4 %copy-start.4 = (bf16[128,1024]{1,0:T(8,128)(2,1)S(1)}, bf16[128,1024]{1,0:T(8,128)(2,1)}, u32[]{:S(2)}) copy-start(bf16[128,1024]{1,0:T(8,128)(2,1)} %get-tuple-element.21) | copy-start | bytes 786436

commit v2 on v1

--- a/solution.py
+++ b/solution.py
@@ -20,6 +20,12 @@
 neg_big = -1e30
 
 
+def shifted(req, dim, off):
+    stride = (16, 4, 1)[dim]
+    at = (req // stride) % 4
+    return req + ((at + off) % 4 - at) * stride
+
+
 def norm_rows(rows, gain):
     widened = rows.astype(jnp.float32)
     mean_square = jnp.mean(widened * widened, axis=-1, keepdims=True)
@@ -29,8 +35,9 @@
 def attention_kernel(
     length_ref, tokens_ref, attn_gain_ref, ffn_gain_ref, freq_ref, routes_ref, scores_ref, replica_ref,
     w_qkv_ref, w_out_ref, k_cache_ref, v_cache_ref,
-    attended_ref, stream_ref, expert_in_ref, appended_ref, meta_ref,
-    w_qkv, w_out, keys, values, queries, heads_out, weight_sems, cache_sems, send_sems, recv_sems,
+    attended_ref, stream_ref, expert_in_ref, appended_ref, plans_ref,
+    w_qkv, w_out, keys, values, queries, heads_out, plans, weight_sems, cache_sems, send_sems, recv_sems,
+    plan_send, plan_recv,
 ):
     rows, width = tokens_ref.shape
     cache_half = k_cache_ref.shape[0]
@@ -58,7 +65,10 @@
 
     barrier = pltpu.get_barrier_semaphore()
     pl.semaphore_signal(barrier, inc=1, device_id=(req, partner), device_id_type=MESH)
-    pl.semaphore_wait(barrier, 1)
+    for dim in range(3):
+        for off in range(1, 4):
+            pl.semaphore_signal(barrier, inc=1, device_id=(shifted(req, dim, off), me), device_id_type=MESH)
+    pl.semaphore_wait(barrier, 10)
 
     def to_partner(src, dst, at):
         return pltpu.make_async_remote_copy(
@@ -71,30 +81,37 @@
     send_k.start()
     send_v.start()
 
-    top = routes_ref.shape[1]
+    top = routes_ref.shape[0]
     lanes = lax.broadcasted_iota(jnp.int32, (rows, 128), 1)
     row_ids = lax.broadcasted_iota(jnp.int32, (rows, 128), 0)
-    experts = replica_ref.shape[1]
-    expert_lane = lax.broadcasted_iota(jnp.int32, (rows, experts), 1)
-    replica = replica_ref[...].astype(jnp.float32)
+    expert_ids = lax.broadcasted_iota(jnp.int32, replica_ref.shape, 0)
+    replica = replica_ref[...]
     routes = routes_ref[...]
     slots = []
-    hits = jnp.zeros((rows, 128), jnp.float32)
+    hits = jnp.zeros((128, rows), jnp.float32)
     for k in range(top):
-        slot = jnp.sum(jnp.where(expert_lane == routes[:, k : k + 1], replica, 0.0), axis=1, keepdims=True)
+        slot = jnp.sum(jnp.where(expert_ids == routes[k : k + 1, :], replica, 0), axis=0, keepdims=True)
         slots.append(slot)
-        hits = hits + jnp.where(lanes == slot.astype(jnp.int32), 1.0, 0.0)
-    earlier = jnp.where(row_ids > lanes, 1.0, 0.0).astype(jnp.bfloat16)
-    before = jnp.dot(earlier, hits.astype(jnp.bfloat16), preferred_element_type=jnp.float32)
+        hits = hits + jnp.where(row_ids == slot, 1.0, 0.0)
+    earlier = jnp.where(row_ids < lanes, 1.0, 0.0).astype(jnp.bfloat16)
+    before = jnp.dot(hits.astype(jnp.bfloat16), earlier, preferred_element_type=jnp.float32)
     scores = scores_ref[...]
-    shares = scores / jnp.sum(scores, axis=1, keepdims=True)
-    table = jnp.zeros((rows, 128), jnp.float32)
-    for k in range(top):
-        rank = jnp.sum(jnp.where(lanes == slots[k].astype(jnp.int32), before, 0.0), axis=1, keepdims=True)
-        table = jnp.where(lanes == k, slots[k], table)
-        table = jnp.where(lanes == top + k, rank, table)
-        table = jnp.where(lanes == 2 * top + k, shares[:, k : k + 1], table)
-    meta_ref[...] = jnp.transpose(table)[: meta_ref.shape[0], :].astype(meta_ref.dtype)
+    shares = scores / jnp.sum(scores, axis=0, keepdims=True)
+    ranks = [jnp.sum(jnp.where(row_ids == slot, before, 0.0), axis=0, keepdims=True) for slot in slots]
+    meta = jnp.concatenate([slot.astype(jnp.float32) for slot in slots] + ranks + [shares, shares], axis=0)
+    meta = meta.astype(jnp.bfloat16)
+    for f in range(3):
+        plans[f, 0, 0] = meta
+    plan_copies = []
+    for f in range(3):
+        for off in range(1, 4):
+            copy = pltpu.make_async_remote_copy(
+                src_ref=plans.at[f, 0, 0], dst_ref=plans.at[f, 0, 4 - off],
+                send_sem=plan_send.at[f, off], recv_sem=plan_recv.at[f, off],
+                device_id=(shifted(req, f, off), me), device_id_type=MESH,
+            )
+            copy.start()
+            plan_copies.append(copy)
 
     normed = norm_rows(tokens_ref[...], attn_gain_ref[...])
     length = length_ref[0]
@@ -140,6 +157,19 @@
                     keep = even_half if kv % 2 == 0 else jnp.logical_not(even_half)
                     queries[kv, member * rows : (member + 1) * rows, :] = jnp.where(keep, source, 0.0).astype(jnp.bfloat16)
 
+    for copy in plan_copies:
+        copy.wait()
+    plan_copies = []
+    for f in range(3):
+        for off in range(1, 4):
+            copy = pltpu.make_async_remote_copy(
+                src_ref=plans.at[f, 0], dst_ref=plans.at[f, 4 - off],
+                send_sem=plan_send.at[f, 3 + off], recv_sem=plan_recv.at[f, 3 + off],
+                device_id=(shifted(req, (f + 1) % 3, off), me), device_id_type=MESH,
+            )
+            copy.start()
+            plan_copies.append(copy)
+
     local_k.wait()
     local_v.wait()
     send_k.wait()
@@ -190,6 +220,9 @@
         product = jnp.dot(attended, w_out[:, cols], preferred_element_type=jnp.float32)
         stream_ref[:, cols] = (tokens_ref[:, cols].astype(jnp.float32) + residual_scale * product).astype(jnp.bfloat16)
     expert_in_ref[...] = norm_rows(stream_ref[...], ffn_gain_ref[...])
+    for copy in plan_copies:
+        copy.wait()
+    plans_ref[...] = plans[...]
 
 
 def attention_call(tokens, attn_gain, w_qkv, w_out, k_cache, v_cache, cache_len, ffn_gain, routes, route_scores, replica_slot):
@@ -206,7 +239,7 @@
     return pl.pallas_call(
         attention_kernel,
         name="attention",
-        out_shape=(shape(rows, width), shape(rows, width), shape(rows, width), shape(rows, 2 * kv_width), shape(32, 128)),
+        out_shape=(shape(rows, width), shape(rows, width), shape(rows, width), shape(rows, 2 * kv_width), shape(3, 4, 4, 32, 128)),
         in_specs=[pl.BlockSpec(memory_space=pltpu.SMEM)] + [vmem] * 7 + [hbm] * 4,
         out_specs=(vmem,) * 5,
         scratch_shapes=[
@@ -216,48 +249,287 @@
             pltpu.VMEM((key_total, kv_width), jnp.bfloat16),
             pltpu.VMEM((KV_HEADS, HEADS // KV_HEADS * rows, 128), jnp.bfloat16),
             pltpu.VMEM((KV_HEADS, HEADS // KV_HEADS * rows, 128), jnp.float32),
+            pltpu.VMEM((3, 4, 4, 32, 128), jnp.bfloat16),
             pltpu.SemaphoreType.DMA((6,)),
             pltpu.SemaphoreType.DMA((2,)),
             pltpu.SemaphoreType.DMA((4,)),
             pltpu.SemaphoreType.DMA((4,)),
+            pltpu.SemaphoreType.DMA((3, 7)),
+            pltpu.SemaphoreType.DMA((3, 7)),
         ],
         compiler_params=pltpu.CompilerParams(
             collective_id=0, has_side_effects=True, vmem_limit_bytes=60 * 1024 * 1024
         ),
-    )(cache_len, tokens, attn_gain[None], ffn_gain[None], freq, routes, route_scores, replica_slot,
+    )(cache_len, tokens, attn_gain[None], ffn_gain[None], freq, routes.T, route_scores.T, replica_slot.T,
       w_qkv, w_out, k_cache[0], v_cache[0])
 
 
-def run_experts(buffer, expert_up, expert_down):
-    gate_up = jnp.einsum("sjcd,jdf->sjcf", buffer, expert_up, preferred_element_type=jnp.float32)
-    hidden_width = expert_down.shape[1]
-    active = (jax.nn.silu(gate_up[..., :hidden_width]) * gate_up[..., hidden_width:]).astype(
-        jnp.bfloat16
-    )
-    return jnp.einsum(
-        "sjcf,jfd->sjcd", active, expert_down, preferred_element_type=jnp.float32
-    ).astype(jnp.bfloat16)
+def source_at(f, oa, ob):
+    return (ob, oa) if f == 2 else (oa, ob)
+
+
+def line_view(ref, crel, f, off):
+    cols = pl.ds(f * 512, 512)
+    every = slice(None)
+    if f == 0:
+        return ref.at[crel, every, every, off, every, cols]
+    if f == 1:
+        return ref.at[crel, off, every, every, every, cols]
+    return ref.at[crel, every, off, every, every, cols]
+
+
+def expert_kernel(
+    expert_in_ref, plans_ref, up_ref, down_ref, mix_ref,
+    up, down, gathered, pick, weigh, outbox, rows_in, rows_out, inbox, sums, sums_b, sums_a, send_a,
+    weight_sems, local_sems, send1, recv1, send2, recv2, send3, recv3, send4, recv4, send5, recv5, send6, recv6,
+):
+    tokens = expert_in_ref.shape[0]
+    req, me = lax.axis_index("req"), lax.axis_index("seq")
+    up_copy = pltpu.make_async_copy(up_ref, up, weight_sems.at[0])
+    down_copy = pltpu.make_async_copy(down_ref, down, weight_sems.at[1])
+    up_copy.start()
+    down_copy.start()
+
+    barrier = pltpu.get_barrier_semaphore()
+    pl.semaphore_signal(barrier, inc=1, device_id=(req, 1 - me), device_id_type=MESH)
+    for dim in range(3):
+        for off in range(1, 4):
+            for core in range(2):
+                pl.semaphore_signal(barrier, inc=1, device_id=(shifted(req, dim, off), core), device_id_type=MESH)
+    pl.semaphore_wait(barrier, 19)
+
+    def send(src, dst, send_sem, recv_sem, dim, off, crel=0):
+        core = me if crel == 0 else 1 - me
+        copy = pltpu.make_async_remote_copy(
+            src_ref=src, dst_ref=dst, send_sem=send_sem, recv_sem=recv_sem,
+            device_id=(shifted(req, dim, off), core), device_id_type=MESH,
+        )
+        copy.start()
+        return copy
+
+    half = tokens // 2
+    low, high = pl.ds(0, half), pl.ds(half, half)
+
+    def block(f, ob, oa):
+        if ob == 0 and oa == 0:
+            return expert_in_ref.at[:, pl.ds(f * 512, 512)]
+        return gathered.at[f, ob, oa]
+
+    first, second = {}, {}
+
+    def start_second(f, oa):
+        b = (f + 1) % 3
+        second[f, oa, 0] = send(block(f, 0, oa), gathered.at[f, 3, oa], send2.at[f, oa, 0], recv2.at[f, oa, 0], b, 1)
+        second[f, oa, 1] = send(block(f, 0, oa), gathered.at[f, 1, oa], send2.at[f, oa, 1], recv2.at[f, oa, 1], b, 3)
+
+    def forward_second(f, oa):
+        b = (f + 1) % 3
+        second[f, oa, 0].wait_recv()
+        second[f, oa, 2] = send(
+            gathered.at[f, 3, oa, low], gathered.at[f, 2, oa, low], send2.at[f, oa, 2], recv2.at[f, oa, 2], b, 1)
+        second[f, oa, 1].wait_recv()
+        second[f, oa, 3] = send(
+            gathered.at[f, 1, oa, high], gathered.at[f, 2, oa, high], send2.at[f, oa, 3], recv2.at[f, oa, 3], b, 3)
+
+    for f in range(3):
+        first[f, 0] = send(block(f, 0, 0), gathered.at[f, 0, 3], send1.at[f, 0], recv1.at[f, 0], f, 1)
+        first[f, 1] = send(block(f, 0, 0), gathered.at[f, 0, 1], send1.at[f, 1], recv1.at[f, 1], f, 3)
+    for f in range(3):
+        start_second(f, 0)
+
+    line_row = lax.broadcasted_iota(jnp.int32, (128, 128), 0)
+    row_crel, row_off, row_rank = line_row // 64, (line_row // 16) % 4, line_row % 16
+
+    def build(f):
+        stride = (16, 4, 1)[(f + 2) % 3]
+        at = (req // stride) % 4
+        target_req = req + ((at + row_off) % 4 - at) * stride
+        target_core = me + row_crel - 2 * me * row_crel
+        target = ((2 * target_req + target_core) * CAP + row_rank).astype(jnp.float32)
+        for ob in range(4):
+            def one(oa, _):
+                plan = plans_ref[f, ob, oa].astype(jnp.float32)
+                position = plan[:8] * CAP + plan[8:16]
+                chosen = jnp.zeros((128, 128), jnp.float32)
+                for k in range(8):
+                    chosen = jnp.where(target == position[k : k + 1, :], plan[16 + k : 17 + k, :], chosen)
+                pick[f, ob, oa] = jnp.where(chosen > 0.0, 1.0, 0.0).astype(jnp.bfloat16)
+                weigh[f, ob, oa] = jnp.transpose(chosen).astype(jnp.bfloat16)
+                return 0
+            lax.fori_loop(0, 4, one, 0)
+
+    def select(f, ob, oa):
+        d1, d2 = source_at(f, oa, ob)
+        rows = jnp.dot(pick[f, ob, oa], block(f, ob, oa)[...], preferred_element_type=jnp.float32)
+        outbox[f, :, :, d1, d2] = rows.astype(jnp.bfloat16).reshape(2, 4, CAP, 512)
+
+    build(0)
+    for f in range(3):
+        first[f, 0].wait_recv()
+        first[f, 2] = send(
+            gathered.at[f, 0, 3, low], gathered.at[f, 0, 2, low], send1.at[f, 2], recv1.at[f, 2], f, 1)
+        first[f, 1].wait_recv()
+        first[f, 3] = send(
+            gathered.at[f, 0, 1, high], gathered.at[f, 0, 2, high], send1.at[f, 3], recv1.at[f, 3], f, 3)
+    for f in range(3):
+        forward_second(f, 0)
+        start_second(f, 3)
+        start_second(f, 1)
+    build(1)
+    for f in range(3):
+        first[f, 2].wait_recv()
+        first[f, 3].wait_recv()
+        start_second(f, 2)
+    build(2)
+    for f in range(3):
+        for oa in range(4):
+            select(f, 0, oa)
+        for ob in (1, 3):
+            select(f, ob, 0)
+    for oa in (3, 1, 2):
+        for f in range(3):
+            forward_second(f, oa)
+        for f in range(3):
+            for ob in (1, 3):
+                select(f, ob, oa)
+    for oa in (0, 3, 1, 2):
+        for f in range(3):
+            second[f, oa, 2].wait_recv()
+            second[f, oa, 3].wait_recv()
+            select(f, 2, oa)
+
+    out, back = {}, {}
+    for crel in range(2):
+        for off in (2, 1, 3, 0):
+            for f in range(3):
+                src, dst = outbox.at[f, crel, off], line_view(rows_in, crel, f, (4 - off) % 4)
+                if crel == 0 and off == 0:
+                    copy = pltpu.make_async_copy(src, dst, local_sems.at[f])
+                    copy.start()
+                else:
+                    copy = send(src, dst, send3.at[f, crel, off], recv3.at[f, crel, off], (f + 2) % 3, off, crel)
+                out[f, crel, off] = copy
+
+    up_copy.wait()
+    down_copy.wait()
+    hidden = down.shape[0]
+    for crel in range(2):
+        for off in range(4):
+            for f in range(3):
+                if crel == 0 and off == 0:
+                    out[f, crel, off].wait()
+                else:
+                    out[f, crel, off].wait_recv()
+
+        def experts(oz, _):
+            rows = rows_in[crel, oz].reshape(256, rows_in.shape[-1])
+            gate = jnp.dot(rows, up[:, :hidden], preferred_element_type=jnp.float32)
+            lift = jnp.dot(rows, up[:, hidden:], preferred_element_type=jnp.float32)
+            active = (gate / (1.0 + jnp.exp(-gate)) * lift).astype(jnp.bfloat16)
+            result = jnp.dot(active, down[...], preferred_element_type=jnp.float32)
+            rows_out[crel, oz] = result.astype(jnp.bfloat16).reshape(rows_out.shape[2:])
+            return 0
+
+        lax.fori_loop(0, 4, experts, 0)
+        for off in (2, 1, 3, 0):
+            for f in range(3):
+                src, dst = line_view(rows_out, crel, f, off), inbox.at[f, crel, (4 - off) % 4]
+                if crel == 0 and off == 0:
+                    copy = pltpu.make_async_copy(src, dst, local_sems.at[3 + f])
+                    copy.start()
+                else:
+                    copy = send(src, dst, send4.at[f, crel, off], recv4.at[f, crel, off], (f + 2) % 3, off, crel)
+                back[f, crel, off] = copy
+
+    for key, copy in back.items():
+        if key[1:] == (0, 0):
+            copy.wait()
+        else:
+            copy.wait_recv()
+
+    def line_sum(f, ob, oa):
+        d1, d2 = source_at(f, oa, ob)
+        rows = inbox[f, :, :, d1, d2].reshape(128, 512)
+        return jnp.dot(weigh[f, ob, oa], rows, preferred_element_type=jnp.float32)
+
+    along_b, along_a = {}, {}
+    for oa in (2, 1, 3, 0):
+        for ob in (2, 1, 3):
+            for f in range(3):
+                sums[f, ob, oa] = line_sum(f, ob, oa).astype(jnp.bfloat16)
+                along_b[f, ob, oa] = send(
+                    sums.at[f, ob, oa], sums_b.at[f, ob - 1, oa],
+                    send5.at[f, ob, oa], recv5.at[f, ob, oa], (f + 1) % 3, ob)
+    for f in range(3):
+        for oa in range(4):
+            sums[f, 0, oa] = line_sum(f, 0, oa).astype(jnp.bfloat16)
+    own = {}
+    for oa in (2, 1, 3, 0):
+        for f in range(3):
+            total = sums[f, 0, oa].astype(jnp.float32)
+            for ob in (2, 1, 3):
+                along_b[f, ob, oa].wait_recv()
+                total = total + sums_b[f, ob - 1, oa].astype(jnp.float32)
+            if oa == 0:
+                own[f] = total
+            else:
+                send_a[f, oa - 1] = total.astype(jnp.bfloat16)
+                along_a[f, oa] = send(
+                    send_a.at[f, oa - 1], sums_a.at[f, oa - 1], send6.at[f, oa], recv6.at[f, oa], f, oa)
+    for f in range(3):
+        total = own[f]
+        for oa in (2, 1, 3):
+            along_a[f, oa].wait_recv()
+            total = total + sums_a[f, oa - 1].astype(jnp.float32)
+        mix_ref[:, f * 512 : (f + 1) * 512] = total.astype(jnp.bfloat16)
+
+    for name, copies in enumerate((first, second, along_b, along_a, out, back)):
+        for key, copy in copies.items():
+            if name < 4 or key[1:] != (0, 0):
+                copy.wait_send()
+
+
+def expert_call(expert_in, plans, expert_up, expert_down):
+    tokens, width = expert_in.shape
+    vmem = pl.BlockSpec(memory_space=pltpu.VMEM)
+    hbm = pl.BlockSpec(memory_space=pl.ANY)
+    half = lambda *dims: pltpu.VMEM(dims, jnp.bfloat16)
+    sems = lambda *dims: pltpu.SemaphoreType.DMA(dims)
+    pairs = lambda *dims: [sems(*dims), sems(*dims)]
+    return pl.pallas_call(
+        expert_kernel,
+        name="experts",
+        out_shape=jax.ShapeDtypeStruct((tokens, width), jnp.bfloat16),
+        in_specs=[vmem, vmem, hbm, hbm],
+        out_specs=vmem,
+        scratch_shapes=[
+            half(*expert_up.shape[1:]),
+            half(*expert_down.shape[1:]),
+            half(3, 4, 4, tokens, 512),
+            half(3, 4, 4, 128, 128),
+            half(3, 4, 4, 128, 128),
+            half(3, 2, 4, 4, 4, CAP, 512),
+            half(2, 4, 4, 4, CAP, width),
+            half(2, 4, 4, 4, CAP, width),
+            half(3, 2, 4, 4, 4, CAP, 512),
+            half(3, 4, 4, tokens, 512),
+            half(3, 3, 4, tokens, 512),
+            half(3, 3, tokens, 512),
+            half(3, 3, tokens, 512),
+            sems(2), sems(6),
+        ]
+        + pairs(3, 4) + pairs(3, 4, 4) + pairs(3, 2, 4) + pairs(3, 2, 4) + pairs(3, 4, 4) + pairs(3, 4),
+        compiler_params=pltpu.CompilerParams(
+            collective_id=1, has_side_effects=True, vmem_limit_bytes=67043328
+        ),
+    )(expert_in, plans, expert_up[0], expert_down[0])
 
 
 def shards(tokens, attn_gain, w_qkv, w_out, k_cache, v_cache, cache_len, ffn_gain, routes, route_scores, replica_slot, expert_up, expert_down):
-    rows, width = tokens.shape
-    attended, stream, expert_in, appended, meta = attention_call(
+    attended, stream, expert_in, appended, plans = attention_call(
         tokens, attn_gain, w_qkv, w_out, k_cache, v_cache, cache_len, ffn_gain, routes, route_scores, replica_slot
     )
-    top = routes.shape[1]
-    slot_total = lax.axis_size("req") * lax.axis_size("seq")
-    wide = meta.astype(jnp.float32)
-    position = wide[:top] * CAP + wide[top : 2 * top]
-    share = wide[2 * top : 3 * top]
-    place_ids = jnp.arange(slot_total * CAP, dtype=jnp.float32)
-    mix = jnp.sum(jnp.where(place_ids[None, :, None] == position[:, None, :], share[:, None, :], 0.0), axis=0)
-    place = (mix > 0).astype(jnp.bfloat16)
-    mix = mix.astype(jnp.bfloat16)
-    outgoing = jnp.dot(place, expert_in, preferred_element_type=jnp.float32).astype(jnp.bfloat16)
-    outgoing = outgoing.reshape(slot_total, 1, CAP, width)
-    exchange = functools.partial(lax.all_to_all, axis_name=("req", "seq"), split_axis=0, concat_axis=0, tiled=True)
-    returned = exchange(run_experts(exchange(outgoing), expert_up, expert_down)).reshape(slot_total * CAP, width)
-    expert_mix = lax.dot_general(mix, returned, (((0,), (0,)), ((), ())), preferred_element_type=jnp.float32).astype(jnp.bfloat16)
+    expert_mix = expert_call(expert_in, plans, expert_up, expert_down)
     return (attended, stream, expert_mix, appended)
 
 

time: 233 us -> 150 us (0.64)
  Pallas kernels: 22.1 us -> 138 us
  blocking collectives: 86.2 us -> 0 us
  waiting for transfers between devices: 75.4 us -> 0 us
  matrix products: 23.8 us -> 0 us
  local copies, waits for them, and re-layouts: 16.1 us -> 9.56 us
  starting transfers between devices: 5.48 us -> 0 us
    pallas_call x0 -> x1, Pallas kernels: none -> 111 us  [expert_call(): pl.pallas_call(expert_kernel, name='experts', out_shape=jax.ShapeDtypeStr...]
    all_to_all x1 -> x0, blocking collectives: 86.2 us -> none  [shards(): exchange(outgoing)]
    all_to_all x1 -> x0, waiting for transfers between devices: 75.4 us -> none  [shards(): exchange(run_experts(exchange(outgoing), expert_up, expert_down))]
    dot_general x4 -> x0, matrix products: 23.8 us -> none  [the longest x1 11.8 us: run_experts(): jnp.einsum('sjcd,jdf->sjcf', buffer, expert_up, preferred_element_type=jn...]
    convert_element_type x1 -> x0, local copies, waits for them, and re-layouts: 6.13 us -> none  [run_experts(): return jnp.einsum('sjcf,jfd->sjcd', active, expert_down, preferred_elemen...]
    all_to_all x1 -> x0, starting transfers between devices: 5.48 us -> none  [shards(): exchange(run_experts(exchange(outgoing), expert_up, expert_down))]
    pallas_call x1, Pallas kernels: 22.1 us -> 26.9 us  [attention_call(): pl.pallas_call(attention_kernel, name='attention', out_shape=(shape(rows,...]
    unnamed x18 -> x4, local copies, waits for them, and re-layouts: 6.51 us -> 6.97 us
  transfers between devices with their start and end apart: 1 -> 0, of which waited for: 1 -> 0; matrix products, arithmetic and copies ran while one was open for 0% -> 0% of each run, Pallas kernels for 0% -> 0%
where the time goes in v2:
time: 150 us; the launch traced here: 149 us
  Pallas kernels  138 us (92%)
  local copies, waits for them, and re-layouts  9.56 us (6%)
    pallas_call x1, Pallas kernels, expert_call(): pl.pallas_call(expert_kernel, name='experts', out_shape=jax.ShapeDtypeStr...  111 us
    pallas_call x1, Pallas kernels, attention_call(): pl.pallas_call(attention_kernel, name='attention', out_shape=(shape(rows,...  26.9 us
    unnamed x4, local copies, waits for them, and re-layouts  6.97 us

profile of v2, /device:TPU:1, one launch (start us, length us, event | category | flops | bytes accessed | tf_op | source)
XLA Modules:
  0.0 149.2 jit_solution(10859953243163114653)
XLA Ops:
  1.3 1.3 broadcast_in_dim.6.attn_gain_ref
  2.6 1.3 broadcast_in_dim.7.ffn_gain_ref
  3.9 26.9 %attention.1 = (bf16[128,1536]{1,0:T(8,128)(2,1)}, bf16[128,1536]{1,0:T(8,128)(2,1)}, bf16[128,1536]{1,0:T(8,128)(2,1)}, bf16[128,1024]{1,0:T(8,128)(2,1)}, bf16[3,4,4,32,128]{4,3,2,1,0:T(8,128)(2,1)}) custom-call(s32[1]{0:T(128)S(6)} %copy.22.length_ref, bf16[128,1536]{1,0:T(8,128)(2,1)} %tokens_ref.1, f32[1,1536]{1,0:T(1,128)} %broadcast_in_dim.6.attn_gain_ref, ...), custom_call_target="tpu_custom_call" | custom-call | tf_op jit(solution)/shard_map/attention/pallas_call | solution.py:239
  30.8 111.4 %experts.1 = bf16[128,1536]{1,0:T(8,128)(2,1)} custom-call(bf16[128,1536]{1,0:T(8,128)(2,1)} %get-tuple-element.11.expert_in_ref, bf16[3,4,4,32,128]{4,3,2,1,0:T(8,128)(2,1)} %get-tuple-element.12.plans_ref, bf16[1536,1024]{1,0:T(8,128)(2,1)} %bitcast.7, bf16[512,1536]{1,0:T(8,128)(2,1)} %bitcast.8), custom_call_target="tpu_custom_call" | custom-call | tf_op jit(solution)/shard_map/experts/pallas_call | solution.py:499
  142.2 1.8 %copy.23 = bf16[128,1536]{1,0:T(8,128)(2,1)} copy(bf16[128,1536]{1,0:T(8,128)(2,1)} %get-tuple-element.18) | data formatting | bytes 786432
  144.0 1.8 %copy.24 = bf16[128,1536]{1,0:T(8,128)(2,1)} copy(bf16[128,1536]{1,0:T(8,128)(2,1)} %get-tuple-element.19) | data formatting | bytes 786432
  145.7 1.8 %copy.25 = bf16[128,1536]{1,0:T(8,128)(2,1)} copy(bf16[128,1536]{1,0:T(8,128)(2,1)} %experts.1) | data formatting | bytes 786432
  147.5 1.7 %copy.26 = bf16[128,1024]{1,0:T(8,128)(2,1)} copy(bf16[128,1024]{1,0:T(8,128)(2,1)} %get-tuple-element.21) | data formatting | bytes 524288

commit v3 on v2

--- a/solution.py
+++ b/solution.py
@@ -113,7 +113,7 @@
             copy.start()
             plan_copies.append(copy)
 
-    normed = norm_rows(tokens_ref[...], attn_gain_ref[...])
+    normed = norm_rows(tokens_ref[...], attn_gain_ref[...].reshape(1, width))
     length = length_ref[0]
     positions = (length + me * rows + row_ids).astype(jnp.float32)
     angles = positions * freq_ref[...]
@@ -219,7 +219,7 @@
         cols = slice(at * chunk, (at + 1) * chunk)
         product = jnp.dot(attended, w_out[:, cols], preferred_element_type=jnp.float32)
         stream_ref[:, cols] = (tokens_ref[:, cols].astype(jnp.float32) + residual_scale * product).astype(jnp.bfloat16)
-    expert_in_ref[...] = norm_rows(stream_ref[...], ffn_gain_ref[...])
+    expert_in_ref[...] = norm_rows(stream_ref[...], ffn_gain_ref[...].reshape(1, width))
     for copy in plan_copies:
         copy.wait()
     plans_ref[...] = plans[...]
@@ -260,7 +260,7 @@
         compiler_params=pltpu.CompilerParams(
             collective_id=0, has_side_effects=True, vmem_limit_bytes=60 * 1024 * 1024
         ),
-    )(cache_len, tokens, attn_gain[None], ffn_gain[None], freq, routes.T, route_scores.T, replica_slot.T,
+    )(cache_len, tokens, attn_gain, ffn_gain, freq, routes.T, route_scores.T, replica_slot.T,
       w_qkv, w_out, k_cache[0], v_cache[0])
 
 
@@ -525,12 +525,40 @@
     )(expert_in, plans, expert_up[0], expert_down[0])
 
 
+def results_kernel(*refs):
+    count = (len(refs) - 2) // 3
+    ins, outs, held = refs[:count], refs[count : 2 * count], refs[2 * count : 3 * count]
+    in_sems, out_sems = refs[3 * count :]
+    loads = [pltpu.make_async_copy(ins[i], held[i], in_sems.at[i]) for i in range(count)]
+    stores = [pltpu.make_async_copy(held[i], outs[i], out_sems.at[i]) for i in range(count)]
+    for load in loads:
+        load.start()
+    for load, store in zip(loads, stores):
+        load.wait()
+        store.start()
+    for store in stores:
+        store.wait()
+
+
+def results_call(*arrays):
+    hbm = pl.BlockSpec(memory_space=pl.ANY)
+    return pl.pallas_call(
+        results_kernel,
+        name="results",
+        out_shape=tuple(jax.ShapeDtypeStruct(a.shape, a.dtype) for a in arrays),
+        in_specs=[hbm] * len(arrays),
+        out_specs=(hbm,) * len(arrays),
+        scratch_shapes=[pltpu.VMEM(a.shape, a.dtype) for a in arrays]
+        + [pltpu.SemaphoreType.DMA((len(arrays),)), pltpu.SemaphoreType.DMA((len(arrays),))],
+    )(*arrays)
+
+
 def shards(tokens, attn_gain, w_qkv, w_out, k_cache, v_cache, cache_len, ffn_gain, routes, route_scores, replica_slot, expert_up, expert_down):
     attended, stream, expert_in, appended, plans = attention_call(
         tokens, attn_gain, w_qkv, w_out, k_cache, v_cache, cache_len, ffn_gain, routes, route_scores, replica_slot
     )
     expert_mix = expert_call(expert_in, plans, expert_up, expert_down)
-    return (attended, stream, expert_mix, appended)
+    return results_call(attended, stream, expert_mix, appended)
 
 
 def solution(mesh):

time: 150 us -> 142 us (0.947)
  local copies, waits for them, and re-layouts: 9.56 us -> 0 us
  Pallas kernels: 138 us -> 140 us
    unnamed x4 -> x0, local copies, waits for them, and re-layouts: 6.97 us -> none
    broadcast_in_dim x2 -> x0, local copies, waits for them, and re-layouts: 2.59 us -> none  [the longest x1 1.3 us: attention_call(): attn_gain[None]]
    pallas_call x0 -> x1, Pallas kernels: none -> 2.16 us  [results_call(): pl.pallas_call(results_kernel, name='results', out_shape=tuple((jax.Shape...]
where the time goes in v3:
time: 142 us
  Pallas kernels  140 us (99%)
  between operations  1.46 us (1%)
    pallas_call x1, Pallas kernels, expert_call(): pl.pallas_call(expert_kernel, name='experts', out_shape=jax.ShapeDtypeStr...  111 us
    pallas_call x1, Pallas kernels, attention_call(): pl.pallas_call(attention_kernel, name='attention', out_shape=(shape(rows,...  26.9 us

profile of v3, /device:TPU:1, one launch (start us, length us, event | category | flops | bytes accessed | tf_op | source)
XLA Modules:
  0.0 141.8 jit_solution(922313215560432836)
XLA Ops:
  1.3 26.9 %attention.1 = (bf16[128,1536]{1,0:T(8,128)(2,1)}, bf16[128,1536]{1,0:T(8,128)(2,1)}, bf16[128,1536]{1,0:T(8,128)(2,1)}, bf16[128,1024]{1,0:T(8,128)(2,1)}, bf16[3,4,4,32,128]{4,3,2,1,0:T(8,128)(2,1)}) custom-call(s32[1]{0:T(128)S(6)} %copy.18.length_ref, bf16[128,1536]{1,0:T(8,128)(2,1)} %tokens_ref.1, f32[1536]{0:T(1024)} %attn_gain_ref.1, ...), custom_call_target="tpu_custom_call" | custom-call | tf_op jit(solution)/shard_map/attention/pallas_call | solution.py:239
  28.2 111.2 %experts.1.refs_2_ = bf16[128,1536]{1,0:T(8,128)(2,1)} custom-call(bf16[128,1536]{1,0:T(8,128)(2,1)} %get-tuple-element.11.expert_in_ref, bf16[3,4,4,32,128]{4,3,2,1,0:T(8,128)(2,1)} %get-tuple-element.12.plans_ref, bf16[1536,1024]{1,0:T(8,128)(2,1)} %bitcast.7, bf16[512,1536]{1,0:T(8,128)(2,1)} %bitcast.8), custom_call_target="tpu_custom_call" | custom-call | tf_op jit(solution)/shard_map/experts/pallas_call | solution.py:499
  139.4 2.2 %results.1 = (bf16[128,1536]{1,0:T(8,128)(2,1)}, bf16[128,1536]{1,0:T(8,128)(2,1)}, bf16[128,1536]{1,0:T(8,128)(2,1)}, bf16[128,1024]{1,0:T(8,128)(2,1)}) custom-call(bf16[128,1536]{1,0:T(8,128)(2,1)} %get-tuple-element.9.refs_0_, bf16[128,1536]{1,0:T(8,128)(2,1)} %get-tuple-element.10.refs_1_, bf16[128,1536]{1,0:T(8,128)(2,1)} %experts.1.refs_2_, ...), custom_call_target="tpu_custom_call" | custom-call | tf_op jit(solution)/shard_map/results/pallas_call | solution.py:545

commit v4 on v3

--- a/solution.py
+++ b/solution.py
@@ -280,7 +280,7 @@
 
 def expert_kernel(
     expert_in_ref, plans_ref, up_ref, down_ref, mix_ref,
-    up, down, gathered, pick, weigh, outbox, rows_in, rows_out, inbox, sums, sums_b, sums_a, send_a,
+    up, down, gathered, pick, weigh, outbox, rows_in, rows_out, inbox, sums, relays_b, sums_b, relays_a, send_a, sums_a,
     weight_sems, local_sems, send1, recv1, send2, recv2, send3, recv3, send4, recv4, send5, recv5, send6, recv6,
 ):
     tokens = expert_in_ref.shape[0]
@@ -452,40 +452,60 @@
         rows = inbox[f, :, :, d1, d2].reshape(128, 512)
         return jnp.dot(weigh[f, ob, oa], rows, preferred_element_type=jnp.float32)
 
-    along_b, along_a = {}, {}
-    for oa in (2, 1, 3, 0):
-        for ob in (2, 1, 3):
-            for f in range(3):
-                sums[f, ob, oa] = line_sum(f, ob, oa).astype(jnp.bfloat16)
-                along_b[f, ob, oa] = send(
-                    sums.at[f, ob, oa], sums_b.at[f, ob - 1, oa],
-                    send5.at[f, ob, oa], recv5.at[f, ob, oa], (f + 1) % 3, ob)
-    for f in range(3):
-        for oa in range(4):
-            sums[f, 0, oa] = line_sum(f, 0, oa).astype(jnp.bfloat16)
-    own = {}
+    relay_b, along_b, relay_a, along_a = {}, {}, {}, {}
     for oa in (2, 1, 3, 0):
         for f in range(3):
-            total = sums[f, 0, oa].astype(jnp.float32)
-            for ob in (2, 1, 3):
-                along_b[f, ob, oa].wait_recv()
-                total = total + sums_b[f, ob - 1, oa].astype(jnp.float32)
-            if oa == 0:
-                own[f] = total
-            else:
-                send_a[f, oa - 1] = total.astype(jnp.bfloat16)
-                along_a[f, oa] = send(
-                    send_a.at[f, oa - 1], sums_a.at[f, oa - 1], send6.at[f, oa], recv6.at[f, oa], f, oa)
+            sums[f, 2, oa] = line_sum(f, 2, oa).astype(jnp.bfloat16)
+            for way, (rows, off) in enumerate(((low, 1), (high, 3))):
+                relay_b[f, oa, way] = send(
+                    sums.at[f, 2, oa, rows], relays_b.at[f, oa, way],
+                    send5.at[f, oa, way], recv5.at[f, oa, way], (f + 1) % 3, off)
+    for oa in (2, 1, 3, 0):
+        for f in range(3):
+            for way, (start, off) in enumerate(((0, 1), (half, 3))):
+                part = line_sum(f, off, oa)
+                relay_b[f, oa, way].wait_recv()
+                passed = relays_b[f, oa, way].astype(jnp.float32)
+                other = part[half - start : tokens - start]
+                sums[f, off, oa, half - start : tokens - start] = other.astype(jnp.bfloat16)
+                sums[f, off, oa, start : start + half] = (part[start : start + half] + passed).astype(jnp.bfloat16)
+                along_b[f, oa, way] = send(
+                    sums.at[f, off, oa], sums_b.at[f, oa, way],
+                    send5.at[f, oa, 2 + way], recv5.at[f, oa, 2 + way], (f + 1) % 3, off)
+
+    def total_b(f, oa):
+        total = line_sum(f, 0, oa)
+        for way in range(2):
+            along_b[f, oa, way].wait_recv()
+            total = total + sums_b[f, oa, way].astype(jnp.float32)
+        return total
+
+    for f in range(3):
+        send_a[f, 2] = total_b(f, 2).astype(jnp.bfloat16)
+        for way, (rows, off) in enumerate(((low, 1), (high, 3))):
+            relay_a[f, way] = send(
+                send_a.at[f, 2, rows], relays_a.at[f, way], send6.at[f, way], recv6.at[f, way], f, off)
+    for way, (start, off) in enumerate(((0, 1), (half, 3))):
+        for f in range(3):
+            part = total_b(f, off)
+            relay_a[f, way].wait_recv()
+            passed = relays_a[f, way].astype(jnp.float32)
+            other = part[half - start : tokens - start]
+            send_a[f, off, half - start : tokens - start] = other.astype(jnp.bfloat16)
+            send_a[f, off, start : start + half] = (part[start : start + half] + passed).astype(jnp.bfloat16)
+            along_a[f, way] = send(
+                send_a.at[f, off], sums_a.at[f, way], send6.at[f, 2 + way], recv6.at[f, 2 + way], f, off)
+    own = [total_b(f, 0) for f in range(3)]
     for f in range(3):
         total = own[f]
-        for oa in (2, 1, 3):
-            along_a[f, oa].wait_recv()
-            total = total + sums_a[f, oa - 1].astype(jnp.float32)
+        for way in range(2):
+            along_a[f, way].wait_recv()
+            total = total + sums_a[f, way].astype(jnp.float32)
         mix_ref[:, f * 512 : (f + 1) * 512] = total.astype(jnp.bfloat16)
 
-    for name, copies in enumerate((first, second, along_b, along_a, out, back)):
-        for key, copy in copies.items():
-            if name < 4 or key[1:] != (0, 0):
+    for copies in (first, second, relay_b, along_b, relay_a, along_a, out, back):
+        for copy in copies.values():
+            if copy.is_remote:
                 copy.wait_send()
 
 
@@ -513,9 +533,11 @@
             half(2, 4, 4, 4, CAP, width),
             half(3, 2, 4, 4, 4, CAP, 512),
             half(3, 4, 4, tokens, 512),
-            half(3, 3, 4, tokens, 512),
-            half(3, 3, tokens, 512),
-            half(3, 3, tokens, 512),
+            half(3, 4, 2, tokens // 2, 512),
+            half(3, 4, 2, tokens, 512),
+            half(3, 2, tokens // 2, 512),
+            half(3, 4, tokens, 512),
+            half(3, 2, tokens, 512),
             sems(2), sems(6),
         ]
         + pairs(3, 4) + pairs(3, 4, 4) + pairs(3, 2, 4) + pairs(3, 2, 4) + pairs(3, 4, 4) + pairs(3, 4),

time: 142 us -> 137 us (0.965)
  Pallas kernels: 140 us -> 135 us
    pallas_call x1, Pallas kernels: 111 us -> 106 us  [expert_call(): pl.pallas_call(expert_kernel, name='experts', out_shape=jax.ShapeDtypeStr...]
where the time goes in v4:
time: 137 us
  Pallas kernels  135 us (99%)
  between operations  1.46 us (1%)
    pallas_call x1, Pallas kernels, expert_call(): pl.pallas_call(expert_kernel, name='experts', out_shape=jax.ShapeDtypeStr...  106 us
    pallas_call x1, Pallas kernels, attention_call(): pl.pallas_call(attention_kernel, name='attention', out_shape=(shape(rows,...  26.9 us

profile of v4, /device:TPU:1, one launch (start us, length us, event | category | flops | bytes accessed | tf_op | source)
XLA Modules:
  0.0 136.5 jit_solution(6188300703479257996)
XLA Ops:
  1.3 26.9 %attention.1 = (bf16[128,1536]{1,0:T(8,128)(2,1)}, bf16[128,1536]{1,0:T(8,128)(2,1)}, bf16[128,1536]{1,0:T(8,128)(2,1)}, bf16[128,1024]{1,0:T(8,128)(2,1)}, bf16[3,4,4,32,128]{4,3,2,1,0:T(8,128)(2,1)}) custom-call(s32[1]{0:T(128)S(6)} %copy.18.length_ref, bf16[128,1536]{1,0:T(8,128)(2,1)} %tokens_ref.1, f32[1536]{0:T(1024)} %attn_gain_ref.1, ...), custom_call_target="tpu_custom_call" | custom-call | tf_op jit(solution)/shard_map/attention/pallas_call | solution.py:239
  28.2 106.0 %experts.1.refs_2_ = bf16[128,1536]{1,0:T(8,128)(2,1)} custom-call(bf16[128,1536]{1,0:T(8,128)(2,1)} %get-tuple-element.11.expert_in_ref, bf16[3,4,4,32,128]{4,3,2,1,0:T(8,128)(2,1)} %get-tuple-element.12.plans_ref, bf16[1536,1024]{1,0:T(8,128)(2,1)} %bitcast.7, bf16[512,1536]{1,0:T(8,128)(2,1)} %bitcast.8), custom_call_target="tpu_custom_call" | custom-call | tf_op jit(solution)/shard_map/experts/pallas_call | solution.py:519
  134.2 2.2 %results.1 = (bf16[128,1536]{1,0:T(8,128)(2,1)}, bf16[128,1536]{1,0:T(8,128)(2,1)}, bf16[128,1536]{1,0:T(8,128)(2,1)}, bf16[128,1024]{1,0:T(8,128)(2,1)}) custom-call(bf16[128,1536]{1,0:T(8,128)(2,1)} %get-tuple-element.9.refs_0_, bf16[128,1536]{1,0:T(8,128)(2,1)} %get-tuple-element.10.refs_1_, bf16[128,1536]{1,0:T(8,128)(2,1)} %experts.1.refs_2_, ...), custom_call_target="tpu_custom_call" | custom-call | tf_op jit(solution)/shard_map/results/pallas_call | solution.py:567
